TPU v7x, 512 devices: a whole 4x8x8 slice. The times are simulated.
512 devices in a mesh: rows: 64 (over y, x, core), rhs: 8 (over z).
Axes of the slice: x: 4, y: 8, z: 8, core: 2. Of those that a mesh axis runs over, the one named last changes fastest.
Arguments:
- right_side: float32 [64, 32768], P('rhs', 'rows'), may hold values from -6 to 6
- tiles: float32 [512, 7, 64, 64], P('rows'), may hold values from -2 to 5.5, as said below
- pivots: float32 [512, 64, 64], P('rows'), may hold values from -0.05 to 0.8, as said below
- columns: int32 [512, 7], P('rows'), may hold values from 0 to 511, as said below
Outputs:
- solution: float32 [64, 32768], P('rhs', 'rows')
- residual: float32 [64, 32768], P('rhs', 'rows')
Inputs may be any that keep to these rules, and one draw needn't show every extreme that they name: columns[i, 0] = i. The other six columns of block row i are i - o and i + o for three offsets o shared by all block rows, the largest of them exactly 8, in an order of the slots drawn for each block row; a column that would fall outside 0 to 511 is i itself. tiles[i, 0] is the diagonal tile of block row i; A is symmetric positive definite: the tile of block row i in a slot whose column j differs from i is the transpose of the tile of block row j in its slot whose column is i. Every pivots[i] is symmetric positive definite.
All inputs are finite; a program needn't handle non-finite values.
Results may differ from a plain program's by a relative error of at most 0.0003.
Values sent between devices are 32-bit elements; how exact they have to be, the bound alone decides.
A program may use at most 64 MiB of HBM per device.

v0:
```python
import jax
import jax.numpy as jnp
from jax import lax
from jax.sharding import PartitionSpec as P

SPAN = 8
ITERS = 2


def passed_along(value, axis, steps):
    count = lax.axis_size(axis)
    first, last = (max(0, -steps), min(count, count - steps))
    return lax.ppermute(value, axis, [(source, source + steps) for source in range(first, last)])


def extended_2(block, sides, width):
    for axis, dim in sides:
        count = lax.axis_size(axis)
        forward = [(i, i + 1) for i in range(count - 1)]
        backward = [(target, source) for source, target in forward]
        low = lax.ppermute(
            lax.slice_in_dim(block, block.shape[dim] - width, None, axis=dim), axis, forward
        )
        high = lax.ppermute(lax.slice_in_dim(block, 0, width, axis=dim), axis, backward)
        block = jnp.concatenate([low, block, high], axis=dim)
    return block


def inner(left, right):
    return jnp.dot(left, right.T, precision=lax.Precision.HIGHEST)


def chol_solve(factor, values):
    middle = lax.linalg.triangular_solve(factor, values, left_side=True, lower=True)
    return lax.linalg.triangular_solve(factor, middle, left_side=True, lower=True, transpose_a=True)


def shards(right_side, tiles, pivots, columns):
    count = right_side.shape[0]
    shard_rows = tiles.shape[0]
    width = tiles.shape[2]
    cells = shard_rows * width
    where_row = lax.axis_index("rows")
    start = where_row * shard_rows
    position = where_row % SPAN
    block_low = (where_row - position) * shard_rows
    block_high = block_low + SPAN * shard_rows
    global_rows = start + jnp.arange(shard_rows, dtype=jnp.int32)
    lower = (columns < global_rows[:, None]) & (columns >= block_low)
    upper = (columns > global_rows[:, None]) & (columns < block_high)
    lower_tiles = tiles * lower[:, :, None, None].astype(tiles.dtype)
    upper_tiles = tiles * upper[:, :, None, None].astype(tiles.dtype)
    forward_cols = jnp.clip(columns - start + shard_rows, 0, 2 * shard_rows - 1)
    backward_cols = jnp.clip(columns - start, 0, 2 * shard_rows - 1)
    halo_cols = columns - start + shard_rows
    from_below = (position != 0).astype(jnp.float32)
    from_above = (position != SPAN - 1).astype(jnp.float32)

    def forward_local(source, incoming):
        extended = jnp.concatenate([incoming, jnp.zeros_like(source)], axis=1)

        def forward_one_row(row, extended):
            picked = jnp.take(extended, forward_cols[row], axis=1)
            summed = jnp.einsum(
                "kab,ckb->ca", lower_tiles[row], picked, precision=lax.Precision.HIGHEST
            )
            remain = source[:, row] - summed
            value = jnp.einsum("ab,cb->ca", pivots[row], remain, precision=lax.Precision.HIGHEST)
            return lax.dynamic_update_slice_in_dim(extended, value[:, None], shard_rows + row, 1)

        extended = lax.fori_loop(0, shard_rows, forward_one_row, extended)
        return extended[:, shard_rows:]

    def backward_local(source, incoming):
        extended = jnp.concatenate([jnp.zeros_like(source), incoming], axis=1)

        def backward_one_row(turn, extended):
            row = shard_rows - 1 - turn
            picked = jnp.take(extended, backward_cols[row], axis=1)
            summed = jnp.einsum(
                "kab,ckb->ca", upper_tiles[row], picked, precision=lax.Precision.HIGHEST
            )
            value = source[:, row] - jnp.einsum(
                "ab,cb->ca", pivots[row], summed, precision=lax.Precision.HIGHEST
            )
            return lax.dynamic_update_slice_in_dim(extended, value[:, None], row, 1)

        extended = lax.fori_loop(0, shard_rows, backward_one_row, extended)
        return extended[:, :shard_rows]

    def precondition(vector):
        source = vector.reshape(count, shard_rows, width)
        lowered = forward_local(source, jnp.zeros_like(source))
        for turn in range(SPAN - 1):
            incoming = passed_along(lowered, "rows", 1) * from_below
            lowered = forward_local(source, incoming)
        result = backward_local(lowered, jnp.zeros_like(lowered))
        for turn in range(SPAN - 1):
            incoming = passed_along(result, "rows", -1) * from_above
            result = backward_local(lowered, incoming)
        return result.reshape(count, cells)

    solution = jnp.zeros_like(right_side)
    residual = right_side
    direction = precondition(residual)
    for turn in range(ITERS):
        blocks = extended_2(direction, (("rows", 1),), cells).reshape(count, 3 * shard_rows, width)
        apply_picked = jnp.take(blocks, halo_cols, axis=1)
        image = jnp.einsum(
            "ikab,cikb->cia", tiles, apply_picked, precision=lax.Precision.HIGHEST
        ).reshape(count, cells)
        every_direction = lax.all_gather(direction, "rhs", axis=0, tiled=True)
        partial_pq = inner(every_direction, image)
        partial_pr = inner(every_direction, residual)
        summed_pq, summed_pr = lax.psum((partial_pq, partial_pr), "rows")
        gram = lax.all_gather(summed_pq, "rhs", axis=1, tiled=True)
        factor = jnp.linalg.cholesky(0.5 * (gram + gram.T))
        alpha = chol_solve(factor, summed_pr)
        change = jnp.dot(alpha.T, every_direction, precision=lax.Precision.HIGHEST)
        solution = solution + change
        if turn + 1 < ITERS:
            every_image = lax.all_gather(image, "rhs", axis=0, tiled=True)
            residual = residual - jnp.dot(alpha.T, every_image, precision=lax.Precision.HIGHEST)
            preconditioned = precondition(residual)
            summed_qz = lax.psum(inner(every_image, preconditioned), "rows")
            beta = -chol_solve(factor, summed_qz)
            direction = preconditioned + jnp.dot(
                beta.T, every_direction, precision=lax.Precision.HIGHEST
            )
        else:
            every_image = lax.all_gather(image, "rhs", axis=0, tiled=True)
            residual = residual - jnp.dot(alpha.T, every_image, precision=lax.Precision.HIGHEST)
    return (solution, residual)


def solution(mesh):
    return jax.shard_map(
        shards,
        mesh=mesh,
        in_specs=(
            P("rhs", "rows"),
            P("rows", None, None, None),
            P("rows", None, None),
            P("rows", None),
        ),
        out_specs=(P("rhs", "rows"), P("rhs", "rows")),
        check_vma=False,
    )
```

profile of v0, /device:TPU:32, one launch (start us, length us, event | category | flops | bytes accessed | tf_op | source)
XLA Modules:
  0.0 1239.9 jit_solution(11222102633937518841)
XLA Ops:
  6.0 16.7 %while.480 = (s32[]{:T(128)}, f32[8,16,64]{2,0,1:T(8,128)S(1)}, f32[8,8,64]{2,0,1:T(8,128)S(1)}, s32[8,7]{1,0:T(8,128)S(1)}, f32[8,7,64,64]{3,2,1,0:T(8,128)}, /...) while((s32[]{:T(128)}, f32[8,16,64]{2,0,1:T(8,128)S(1)}, ...), condition=%wide.region_1.3_spmd, body=%wide.region_0.2_spmd.sunk | while | flops 3150896 | bytes 322845 | solution.py:71
  31.3 16.7 %while.481 = (s32[]{:T(128)}, f32[8,16,64]{2,0,1:T(8,128)S(1)}, f32[8,8,64]{2,0,1:T(8,128)S(1)}, s32[8,7]{1,0:T(8,128)S(1)}, f32[8,7,64,64]{3,2,1,0:T(8,128)}, /...) while((s32[]{:T(128)}, f32[8,16,64]{2,0,1:T(8,128)S(1)}, ...), condition=%wide.region_3.5_spmd, body=%wide.region_2.4_spmd.sunk | while | flops 3150896 | bytes 322845 | solution.py:71
  50.0 6.6 collective-permute-done.1
  56.6 16.7 %while.482 = (s32[]{:T(128)}, f32[8,16,64]{2,0,1:T(8,128)S(1)}, f32[8,8,64]{2,0,1:T(8,128)S(1)}, s32[8,7]{1,0:T(8,128)S(1)}, f32[8,7,64,64]{3,2,1,0:T(8,128)}, /...) while((s32[]{:T(128)}, f32[8,16,64]{2,0,1:T(8,128)S(1)}, ...), condition=%wide.region_5.7_spmd, body=%wide.region_4.6_spmd.sunk | while | flops 3150896 | bytes 322845 | solution.py:71
  75.3 6.6 collective-permute-done.2
  81.9 16.7 %while.483 = (s32[]{:T(128)}, f32[8,16,64]{2,0,1:T(8,128)S(1)}, f32[8,8,64]{2,0,1:T(8,128)S(1)}, s32[8,7]{1,0:T(8,128)S(1)}, f32[8,7,64,64]{3,2,1,0:T(8,128)}, /...) while((s32[]{:T(128)}, f32[8,16,64]{2,0,1:T(8,128)S(1)}, ...), condition=%wide.region_7.9_spmd, body=%wide.region_6.8_spmd.sunk | while | flops 3150896 | bytes 322845 | solution.py:71
  100.6 6.6 collective-permute-done.3
  107.2 16.7 %while.484 = (s32[]{:T(128)}, f32[8,16,64]{2,0,1:T(8,128)S(1)}, f32[8,8,64]{2,0,1:T(8,128)S(1)}, s32[8,7]{1,0:T(8,128)S(1)}, f32[8,7,64,64]{3,2,1,0:T(8,128)}, /...) while((s32[]{:T(128)}, f32[8,16,64]{2,0,1:T(8,128)S(1)}, ...), condition=%wide.region_9.11_spmd, body=%wide.region_8.10_spmd.sunk | while | flops 3150896 | bytes 322845 | solution.py:71
  125.9 6.6 collective-permute-done.4
  132.5 16.7 %while.485 = (s32[]{:T(128)}, f32[8,16,64]{2,0,1:T(8,128)S(1)}, f32[8,8,64]{2,0,1:T(8,128)S(1)}, s32[8,7]{1,0:T(8,128)S(1)}, f32[8,7,64,64]{3,2,1,0:T(8,128)}, /...) while((s32[]{:T(128)}, f32[8,16,64]{2,0,1:T(8,128)S(1)}, ...), condition=%wide.region_11.13_spmd, body=%wide.region_10.12_spmd.sunk | while | flops 3150896 | bytes 322845 | solution.py:71
  151.2 6.6 collective-permute-done.5
  157.8 16.7 %while.486 = (s32[]{:T(128)}, f32[8,16,64]{2,0,1:T(8,128)S(1)}, f32[8,8,64]{2,0,1:T(8,128)S(1)}, s32[8,7]{1,0:T(8,128)S(1)}, f32[8,7,64,64]{3,2,1,0:T(8,128)}, /...) while((s32[]{:T(128)}, f32[8,16,64]{2,0,1:T(8,128)S(1)}, ...), condition=%wide.region_13.15_spmd, body=%wide.region_12.14_spmd.sunk | while | flops 3150896 | bytes 322845 | solution.py:71
  176.5 6.6 collective-permute-done.6
  183.1 16.7 %while.487 = (s32[]{:T(128)}, f32[8,16,64]{2,0,1:T(8,128)S(1)}, f32[8,8,64]{2,0,1:T(8,128)S(1)}, s32[8,7]{1,0:T(8,128)S(1)}, f32[8,7,64,64]{3,2,1,0:T(8,128)}, /...) while((s32[]{:T(128)}, f32[8,16,64]{2,0,1:T(8,128)S(1)}, ...), condition=%wide.region_15.17_spmd, body=%wide.region_14.16_spmd.sunk | while | flops 3150896 | bytes 322845 | solution.py:71
  199.9 9.2 while.488
  212.6 9.2 while.489
  221.8 7.0 collective-permute-start.8
  230.4 9.2 while.490
  239.6 7.0 collective-permute-start.9
  248.2 9.2 while.491
  257.4 7.0 collective-permute-start.10
  266.0 9.2 while.492
  275.2 7.0 collective-permute-start.11
  283.8 9.2 while.493
  293.0 7.0 collective-permute-start.12
  301.6 9.2 while.494
  310.8 7.0 collective-permute-start.13
  319.4 9.2 while.495
  330.6 7.0 collective-permute-start.15
  337.6 30.9 %all_gather.18 = f32[64,512]{1,0:T(8,128)S(1)} all-gather(f32[8,512]{1,0:T(8,128)S(1)} %reshape.66), channel_id=1, replica_groups=mesh['rows'=64,'rhs'=8] {'rhs'}, dimensions={0}, use_global_device_ids=true | all-gather | bytes 147456 | tf_op jit(solution)/shard_map/all_gather | solution.py:112
  373.2 24.6 %all_gather.20 = f32[64,512]{1,0:T(8,128)S(1)} all-gather(f32[8,512]{1,0:T(8,128)S(1)} %reshape.67), channel_id=1, replica_groups=mesh['rows'=64,'rhs'=8] {'rhs'}, dimensions={0}, use_global_device_ids=true | all-gather | bytes 147456 | tf_op jit(solution)/shard_map/all_gather | solution.py:122
  397.8 126.1 %all-reduce.29 = (f32[64,8]{0,1:T(8,128)S(1)}, f32[64,8]{0,1:T(8,128)S(1)}) all-reduce(f32[64,8]{0,1:T(8,128)S(1)} %fusion.476, f32[64,8]{0,1:T(8,128)S(1)} %fusion.475), channel_id=1, replica_groups=mesh['rows'=64,'rhs'=8] {'rows'}, use_global_device_ids=true, to_apply=%region_35.39 | all-reduce | flops 1024 | bytes 8192 | tf_op jit(solution)/shard_map/psum | solution.py:115
  523.9 24.5 %all_gather.19 = f32[64,64]{0,1:T(8,128)S(1)} all-gather(f32[64,8]{0,1:T(8,128)S(1)} %get-tuple-element.5610), channel_id=1, replica_groups=mesh['rows'=64,'rhs'=8] {'rhs'}, dimensions={1}, use_global_device_ids=true | all-gather | bytes 18432 | tf_op jit(solution)/shard_map/all_gather | solution.py:116
  561.3 16.7 %while.496 = (s32[]{:T(128)}, f32[8,16,64]{2,0,1:T(8,128)S(1)}, f32[8,8,64]{2,0,1:T(8,128)S(1)}, s32[8,7]{1,0:T(8,128)S(1)}, f32[8,7,64,64]{3,2,1,0:T(8,128)}, /...) while((s32[]{:T(128)}, f32[8,16,64]{2,0,1:T(8,128)S(1)}, ...), condition=%wide.region_37.43_spmd, body=%wide.region_36.42_spmd.sunk | while | flops 3150896 | bytes 322845 | solution.py:71
  586.6 16.7 %while.497 = (s32[]{:T(128)}, f32[8,16,64]{2,0,1:T(8,128)S(1)}, f32[8,8,64]{2,0,1:T(8,128)S(1)}, s32[8,7]{1,0:T(8,128)S(1)}, f32[8,7,64,64]{3,2,1,0:T(8,128)}, /...) while((s32[]{:T(128)}, f32[8,16,64]{2,0,1:T(8,128)S(1)}, ...), condition=%wide.region_39.45_spmd, body=%wide.region_38.44_spmd.sunk | while | flops 3150896 | bytes 322845 | solution.py:71
  605.3 6.6 collective-permute-done.17
  611.9 16.7 %while.498 = (s32[]{:T(128)}, f32[8,16,64]{2,0,1:T(8,128)S(1)}, f32[8,8,64]{2,0,1:T(8,128)S(1)}, s32[8,7]{1,0:T(8,128)S(1)}, f32[8,7,64,64]{3,2,1,0:T(8,128)}, /...) while((s32[]{:T(128)}, f32[8,16,64]{2,0,1:T(8,128)S(1)}, ...), condition=%wide.region_41.47_spmd, body=%wide.region_40.46_spmd.sunk | while | flops 3150896 | bytes 322845 | solution.py:71
  630.6 6.6 collective-permute-done.18
  637.2 16.7 %while.499 = (s32[]{:T(128)}, f32[8,16,64]{2,0,1:T(8,128)S(1)}, f32[8,8,64]{2,0,1:T(8,128)S(1)}, s32[8,7]{1,0:T(8,128)S(1)}, f32[8,7,64,64]{3,2,1,0:T(8,128)}, /...) while((s32[]{:T(128)}, f32[8,16,64]{2,0,1:T(8,128)S(1)}, ...), condition=%wide.region_43.49_spmd, body=%wide.region_42.48_spmd.sunk | while | flops 3150896 | bytes 322845 | solution.py:71
  662.5 16.7 %while.500 = (s32[]{:T(128)}, f32[8,16,64]{2,0,1:T(8,128)S(1)}, f32[8,8,64]{2,0,1:T(8,128)S(1)}, s32[8,7]{1,0:T(8,128)S(1)}, f32[8,7,64,64]{3,2,1,0:T(8,128)}, /...) while((s32[]{:T(128)}, f32[8,16,64]{2,0,1:T(8,128)S(1)}, ...), condition=%wide.region_45.51_spmd, body=%wide.region_44.50_spmd.sunk | while | flops 3150896 | bytes 322845 | solution.py:71
  687.8 16.7 %while.501 = (s32[]{:T(128)}, f32[8,16,64]{2,0,1:T(8,128)S(1)}, f32[8,8,64]{2,0,1:T(8,128)S(1)}, s32[8,7]{1,0:T(8,128)S(1)}, f32[8,7,64,64]{3,2,1,0:T(8,128)}, /...) while((s32[]{:T(128)}, f32[8,16,64]{2,0,1:T(8,128)S(1)}, ...), condition=%wide.region_47.53_spmd, body=%wide.region_46.52_spmd.sunk | while | flops 3150896 | bytes 322845 | solution.py:71
  706.5 6.6 collective-permute-done.21
  713.1 16.7 %while.502 = (s32[]{:T(128)}, f32[8,16,64]{2,0,1:T(8,128)S(1)}, f32[8,8,64]{2,0,1:T(8,128)S(1)}, s32[8,7]{1,0:T(8,128)S(1)}, f32[8,7,64,64]{3,2,1,0:T(8,128)}, /...) while((s32[]{:T(128)}, f32[8,16,64]{2,0,1:T(8,128)S(1)}, ...), condition=%wide.region_49.55_spmd, body=%wide.region_48.54_spmd.sunk | while | flops 3150896 | bytes 322845 | solution.py:71
  738.4 16.7 %while.503 = (s32[]{:T(128)}, f32[8,16,64]{2,0,1:T(8,128)S(1)}, f32[8,8,64]{2,0,1:T(8,128)S(1)}, s32[8,7]{1,0:T(8,128)S(1)}, f32[8,7,64,64]{3,2,1,0:T(8,128)}, /...) while((s32[]{:T(128)}, f32[8,16,64]{2,0,1:T(8,128)S(1)}, ...), condition=%wide.region_51.57_spmd, body=%wide.region_50.56_spmd.sunk | while | flops 3150896 | bytes 322845 | solution.py:71
  755.2 9.2 while.504
  767.9 9.2 while.505
  777.1 7.0 collective-permute-start.24
  785.7 9.2 while.506
  794.9 7.0 collective-permute-start.25
  803.5 9.2 while.507
  812.7 7.0 collective-permute-start.26
  821.3 9.2 while.508
  830.5 7.0 collective-permute-start.27
  839.1 9.2 while.509
  848.3 7.0 collective-permute-start.28
  856.9 9.2 while.510
  866.1 7.0 collective-permute-start.29
  874.7 9.2 while.511
  884.2 129.3 %psum.37 = f32[64,8]{0,1:T(8,128)S(1)} all-reduce(f32[64,8]{0,1:T(8,128)S(1)} %fusion.478), channel_id=1, replica_groups=mesh['rows'=64,'rhs'=8] {'rows'}, use_global_device_ids=true, to_apply=%region_68.74 | all-reduce | flops 512 | bytes 4096 | tf_op jit(solution)/shard_map/psum | solution.py:125
  1015.9 7.0 collective-permute-start.31
  1022.8 24.6 %all_gather.21 = f32[64,512]{1,0:T(8,128)S(1)} all-gather(f32[8,512]{1,0:T(8,128)S(1)} %convolution_add_fusion.1), channel_id=1, replica_groups=mesh['rows'=64,'rhs'=8] {'rhs'}, dimensions={0}, use_global_device_ids=true | all-gather | bytes 147456 | tf_op jit(solution)/shard_map/all_gather | solution.py:112
  1050.5 24.6 %all_gather.23 = f32[64,512]{1,0:T(8,128)S(1)} all-gather(f32[8,512]{1,0:T(8,128)S(1)} %reshape.71), channel_id=1, replica_groups=mesh['rows'=64,'rhs'=8] {'rhs'}, dimensions={0}, use_global_device_ids=true | all-gather | bytes 147456 | tf_op jit(solution)/shard_map/all_gather | solution.py:131
  1075.2 126.1 %all-reduce.28 = (f32[64,8]{0,1:T(8,128)S(1)}, f32[64,8]{0,1:T(8,128)S(1)}) all-reduce(f32[64,8]{0,1:T(8,128)S(1)} %fusion.480, f32[64,8]{0,1:T(8,128)S(1)} %fusion.479), channel_id=1, replica_groups=mesh['rows'=64,'rhs'=8] {'rows'}, use_global_device_ids=true, to_apply=%region_70.76 | all-reduce | flops 1024 | bytes 8192 | tf_op jit(solution)/shard_map/psum | solution.py:115
  1201.3 24.5 %all_gather.22 = f32[64,64]{0,1:T(8,128)S(1)} all-gather(f32[64,8]{0,1:T(8,128)S(1)} %get-tuple-element.5608), channel_id=1, replica_groups=mesh['rows'=64,'rhs'=8] {'rhs'}, dimensions={1}, use_global_device_ids=true | all-gather | bytes 18432 | tf_op jit(solution)/shard_map/all_gather | solution.py:116
  (1483 shorter events, 539.3 us)
Async XLA Ops:
  2.9 3.1 copy-start
  22.7 8.6 collective-permute-start
  48.0 8.6 collective-permute-start.1
  73.3 8.6 collective-permute-start.2
  98.6 8.6 collective-permute-start.3
  123.9 8.6 collective-permute-start.4
  149.2 8.6 collective-permute-start.5
  174.5 8.6 collective-permute-start.6
  209.1 3.5 collective-permute-start.7
  221.8 8.6 collective-permute-start.8
  239.6 8.6 collective-permute-start.9
  257.4 8.6 collective-permute-start.10
  275.2 8.6 collective-permute-start.11
  293.0 8.6 collective-permute-start.12
  310.8 57.8 %copy-start.2 = (f32[8,512]{1,0:T(8,128)S(1)}, f32[8,512]{1,0:T(8,128)}, u32[]{:S(2)}) copy-start(f32[8,512]{1,0:T(8,128)} %param.77) | copy-start | bytes 49156
  310.8 8.6 collective-permute-start.13
  328.7 40.0 %collective-permute-start.14 = (f32[8,512]{1,0:T(8,128)S(1)}, f32[8,512]{1,0:T(8,128)S(1)}, u32[]{:S(2)}, u32[]{:S(2)}) collective-permute-start(f32[8,512]{1,0:T(8,128)S(1)} %reshape.66), channel_id=1, source_target_pairs={{0,8},{8,16},{16,24},{24,32},{32,40},{40,48},{48,56},{56,64},{64,7... | collective-permute-start | bytes 49160 | tf_op jit(solution)/shard_map/ppermute | solution.py:21
  330.6 38.2 %collective-permute-start.15 = (f32[8,512]{1,0:T(8,128)S(1)}, f32[8,512]{1,0:T(8,128)S(1)}, u32[]{:S(2)}, u32[]{:S(2)}) collective-permute-start(f32[8,512]{1,0:T(8,128)S(1)} %reshape.66), channel_id=1, source_target_pairs={{8,0},{16,8},{24,16},{32,24},{40,32},{48,40},{56,48},{64,56},{72,6... | collective-permute-start | bytes 49160 | tf_op jit(solution)/shard_map/ppermute | solution.py:24
  578.0 8.6 collective-permute-start.16
  603.3 8.6 collective-permute-start.17
  628.6 8.6 collective-permute-start.18
  653.9 8.6 collective-permute-start.19
  679.2 8.6 collective-permute-start.20
  704.5 8.6 collective-permute-start.21
  729.8 8.6 collective-permute-start.22
  764.4 3.5 collective-permute-start.23
  777.1 8.6 collective-permute-start.24
  794.9 8.6 collective-permute-start.25
  812.7 8.6 collective-permute-start.26
  830.5 8.6 collective-permute-start.27
  848.3 8.6 collective-permute-start.28
  866.1 8.6 collective-permute-start.29
  883.9 164.5 %copy-start.1 = (f32[8,7,64,64]{3,2,1,0:T(8,128)S(1)}, f32[8,7,64,64]{3,2,1,0:T(8,128)}, u32[]{:S(2)}) copy-start(f32[8,7,64,64]{3,2,1,0:T(8,128)} %param.78) | copy-start | bytes 2752516
  1013.9 33.6 %collective-permute-start.30 = (f32[8,512]{1,0:T(8,128)S(1)}, f32[8,512]{1,0:T(8,128)S(1)}, u32[]{:S(2)}, u32[]{:S(2)}) collective-permute-start(f32[8,512]{1,0:T(8,128)S(1)} %convolution_add_fusion.1), channel_id=1, source_target_pairs={{0,8},{8,16},{16,24},{24,32},{32,40},{40,48},{48,56},{56,64},{64,7... | collective-permute-start | bytes 49160 | tf_op jit(solution)/shard_map/ppermute | solution.py:21
  1015.9 31.8 %collective-permute-start.31 = (f32[8,512]{1,0:T(8,128)S(1)}, f32[8,512]{1,0:T(8,128)S(1)}, u32[]{:S(2)}, u32[]{:S(2)}) collective-permute-start(f32[8,512]{1,0:T(8,128)S(1)} %convolution_add_fusion.1), channel_id=1, source_target_pairs={{8,0},{16,8},{24,16},{32,24},{40,32},{48,40},{56,48},{64,56},{72,6... | collective-permute-start | bytes 49160 | tf_op jit(solution)/shard_map/ppermute | solution.py:24
where the time goes:
time: 1240 us
  blocking collectives  535 us (43%)
  matrix products  265 us (21%)
  local copies, waits for them, and re-layouts  146 us (12%)
  starting transfers between devices  133 us (11%)
  waiting for transfers between devices  114 us (9%)
  other arithmetic  39.3 us (3%)
    psum x2, blocking collectives, shards(): summed_pq, summed_pr = lax.psum((partial_pq, partial_pr), 'rows')  252 us
    dot_general x128, matrix products, forward_one_row(): jnp.einsum('kab,ckb->ca', lower_tiles[row], picked, precision=lax.Precisi...  162 us
    psum x1, blocking collectives, shards(): summed_qz = lax.psum(inner(every_image, preconditioned), 'rows')  129 us
    ppermute x28, starting transfers between devices, passed_along(): lax.ppermute(value, axis, [(source, source + steps) for source in range(f...  115 us
    ppermute x28, waiting for transfers between devices, passed_along(): lax.ppermute(value, axis, [(source, source + steps) for source in range(f...  114 us
    gather x128, local copies, waits for them, and re-layouts, forward_one_row(): picked = jnp.take(extended, forward_cols[row], axis=1)  70.9 us
    gather x128, local copies, waits for them, and re-layouts, backward_one_row(): picked = jnp.take(extended, backward_cols[row], axis=1)  70.9 us
    all_gather x2, blocking collectives, shards(): every_direction = lax.all_gather(direction, 'rhs', axis=0, tiled=True)  55.5 us
  transfers between devices with their start and end apart: 32, of which 28 were waited for; matrix products, arithmetic and copies ran while one was open for 0% of the time, Pallas kernels for 0%

commit v1 on v0

v1 whole, which is shorter than its diff:
```python
import functools

import jax
import jax.numpy as jnp
from jax import lax
from jax.experimental import pallas as pl
from jax.experimental.pallas import tpu as pltpu
from jax.sharding import PartitionSpec as P

SPAN = 8
BF, F32 = jnp.bfloat16, jnp.float32
MIB = 1 << 20
VMEM = pl.BlockSpec(memory_space=pltpu.VMEM)
SMEM = pl.BlockSpec(memory_space=pltpu.SMEM)


def parts(x, n):
    out = []
    for _ in range(n):
        high = x.astype(BF)
        out.append(high)
        x = x - high.astype(F32)
    return out


def dot(a, b):
    return jnp.dot(a, b, preferred_element_type=F32)


def mul(a, b):
    (ah, al), (bh, bl) = parts(a, 2), parts(b, 2)
    return dot(ah, bh) + (dot(ah, bl) + dot(al, bh))


def times(x, weights):
    n = x.shape[0]
    count = len(weights)
    stack = jnp.concatenate([p.astype(F32) for p in parts(x, count)], axis=0)
    if count * n % 16:
        stack = jnp.concatenate([stack, jnp.zeros((16 - count * n % 16, x.shape[1]), F32)], axis=0)
    stack = stack.astype(BF)
    total = None
    for w in reversed(weights):
        y = dot(stack, w)
        for i in reversed(range(count)):
            y_i = y[i * n : (i + 1) * n]
            total = y_i if total is None else total + y_i
    return total


def setup_kernel(cols, tiles, pivots, dh, dm, dl, nh, nl, th, tl, sh, sl, dense, pf):
    rows, slots, bs = tiles.shape[0], tiles.shape[1], tiles.shape[2]
    cells = rows * bs
    half = cells // 2
    start = lax.axis_index("rows") * rows
    dense[...] = jnp.zeros(dense.shape, F32)
    for i in range(rows):
        for k in range(slots):
            j = cols[i, k] - start + rows
            at = (pl.ds(pl.multiple_of(j * bs, bs), bs), slice(i * bs, (i + 1) * bs))
            dense[at] = dense[at] + tiles[i, k].T
    for at in range(3):
        part = slice(at * cells, (at + 1) * cells)
        for ref, p in zip((dh, dm, dl), parts(dense[part], 3)):
            ref[part] = p

    def block_diagonal(first):
        zero = jnp.zeros((bs, bs), F32)
        count = half // bs
        return jnp.concatenate(
            [
                jnp.concatenate([pivots[first + i] if i == j else zero for j in range(count)], axis=1)
                for i in range(count)
            ],
            axis=0,
        )

    pa, pb = block_diagonal(0), block_diagonal(rows // 2)
    row = lax.broadcasted_iota(jnp.int32, (half, half), 0)
    col = lax.broadcasted_iota(jnp.int32, (half, half), 1)
    same_pair = row // (2 * bs) == col // (2 * bs)
    eye = (row == col).astype(F32)
    lower = row // bs > col // bs

    def inverse(block):
        first = jnp.where(same_pair, block, 0.0)
        rest = block - first
        f = eye - first
        return f - mul(mul(f, rest), f)

    o = cells
    ga = mul(jnp.where(lower, dense[o : o + half, 0:half], 0.0), pa)
    gb = mul(jnp.where(lower, dense[o + half : o + cells, half:cells], 0.0), pb)
    gx = mul(dense[o + half : o + cells, 0:half], pa)
    fa, fb = inverse(ga), inverse(gb)
    fx = -mul(mul(fb, gx), fa)
    pf[0:half, 0:half] = mul(pa, fa)
    pf[0:half, half:cells] = jnp.zeros((half, half), F32)
    pf[half:cells, 0:half] = mul(pb, fx)
    pf[half:cells, half:cells] = mul(pb, fb)
    right = pf[...]
    n = mul(dense[2 * cells : 3 * cells], right)
    nh[...], nl[...] = parts(n, 2)
    th[...], tl[...] = parts(n.T, 2)
    fxt, fbt = fx.T, fb.T
    low = mul(fbt, right[half:cells])
    sh[half:cells], sl[half:cells] = parts(low, 2)
    high = mul(fxt, right[half:cells])
    corner = mul(fa.T, right[0:half, 0:half])
    high = jnp.concatenate([high[:, 0:half] + corner, high[:, half:cells]], axis=1)
    sh[0:half], sl[0:half] = parts(high, 2)


def setup(cols, tiles, pivots):
    rows, _, bs, _ = tiles.shape
    cells = rows * bs
    shapes = [(3 * cells, cells)] * 3 + [(cells, cells)] * 6
    return pl.pallas_call(
        setup_kernel,
        out_shape=[jax.ShapeDtypeStruct(s, BF) for s in shapes],
        in_specs=[SMEM, VMEM, VMEM],
        out_specs=[VMEM] * 9,
        scratch_shapes=[pltpu.VMEM((3 * cells, cells), F32), pltpu.VMEM((cells, cells), F32)],
        compiler_params=pltpu.CompilerParams(vmem_limit_bytes=40 * MIB),
    )(cols, tiles, pivots)


def krylov_kernel(
    nr, nz,
    r, dh, dm, dl, nh, nl, th, tl, sh, sl,
    v_out, w_out, k_out, r_out,
    va, wa, fsrc, fdst, above, below, c, red_x, red_y, red_z,
    f_send, f_recv, b_send, b_recv, h_send, h_recv,
    z_send, z_recv, x_send, x_recv, y_send, y_recv, k_send, k_recv,
):
    me, mz = lax.axis_index("rows"), lax.axis_index("rhs")
    pos, where = lax.rem(me, SPAN), lax.div(me, SPAN)
    ny = nr // SPAN
    first, last = pos == 0, pos == SPAN - 1
    cells = r.shape[1]

    def x_peer(o):
        return (where * SPAN + lax.rem(pos + o, SPAN), mz)

    def y_peer(o):
        return (lax.rem(where + o, ny) * SPAN + pos, mz)

    def z_peer(o):
        return (me, lax.rem(mz + o, nz))

    barrier = pltpu.get_barrier_semaphore()

    def hello(device):
        pl.semaphore_signal(barrier, inc=1, device_id=device, device_id_type=pl.DeviceIdType.MESH)

    for o in range(1, SPAN):
        hello(x_peer(o))
    for o in range(1, ny):
        hello(y_peer(o))
    for o in range(1, nz):
        hello(z_peer(o))
    from_before, to_next = first & (me > 0), last & (me < nr - 1)

    @pl.when(from_before)
    def _():
        hello((me - 1, mz))

    @pl.when(to_next)
    def _():
        hello((me + 1, mz))

    edges = from_before.astype(jnp.int32) + to_next.astype(jnp.int32)
    pl.semaphore_wait(barrier, SPAN - 1 + ny - 1 + nz - 1 + edges)

    def copy(src, dst, send, recv, device):
        return pltpu.make_async_remote_copy(
            src_ref=src, dst_ref=dst, send_sem=send, recv_sem=recv,
            device_id=device, device_id_type=pl.DeviceIdType.MESH,
        )

    def to_z(array, m, kind):
        return [
            copy(array.at[mz, m], array.at[mz, m], z_send.at[kind, o - 1], z_recv.at[kind, o - 1], z_peer(o))
            for o in range(1, nz)
        ]

    def spread(array, at, send, recv, peer, count):
        return [
            copy(array.at[at], array.at[at], send.at[o - 1], recv.at[o - 1], peer(o)) for o in range(1, count)
        ]

    begun = []
    has_before, has_next = me > 0, me < nr - 1

    @pl.when(me == 0)
    def _():
        below[...] = jnp.zeros(below.shape, F32)

    @pl.when(me == nr - 1)
    def _():
        above[...] = jnp.zeros(above.shape, F32)

    n_parts, t_parts, s_parts = (nh, nl), (th, tl), (sh, sl)

    def values(refs, rows=slice(None)):
        return [ref[rows] for ref in refs]

    for m in range(2):
        source = r if m == 0 else wa.at[mz, 0]
        ahead = copy(fsrc.at[m], fdst.at[m], f_send.at[m], f_recv.at[m], (me + 1, mz))
        back = copy(va.at[mz, m], above.at[m], b_send.at[m], b_recv.at[m], (me - 1, mz))
        on = copy(va.at[mz, m], below.at[m], h_send.at[m], h_recv.at[m], (me + 1, mz))

        @pl.when(first)
        def _():
            c[...] = source[...]

        @pl.when(jnp.logical_not(first))
        def _():
            ahead.wait_recv()
            c[...] = source[...] - fdst[m]

        @pl.when(jnp.logical_not(last))
        def _():
            fsrc[m] = times(c[...], values(t_parts))
            ahead.start()

        c[...] = times(c[...], values(s_parts))

        @pl.when(last)
        def _():
            va[mz, m] = c[...]

        @pl.when(jnp.logical_not(last))
        def _():
            back.wait_recv()
            va[mz, m] = c[...] - times(above[m], values(n_parts))

        @pl.when(has_before)
        def _():
            back.start()

        @pl.when(has_next)
        def _():
            on.start()

        sent = to_z(va, m, 2 * m)
        for s in sent:
            s.start()
        begun += sent

        d = (dh, dm, dl)
        q = times(va[mz, m], values(d, slice(cells, 2 * cells)))

        @pl.when(to_next)
        def _():
            back.wait_recv()

        q = q + times(above[m], values(d, slice(2 * cells, 3 * cells)))

        @pl.when(has_before)
        def _():
            on.wait_recv()

        wa[mz, m] = q + times(below[m], values(d, slice(0, cells)))
        sent = to_z(wa, m, 2 * m + 1)
        for s in sent:
            s.start()
        begun += sent

    for m in range(2):
        for s in to_z(va, m, 2 * m):
            s.wait_recv()
    left = jnp.concatenate([wa[mz, 0], wa[mz, 1], r[...]], axis=0)
    right = va[...].reshape(nz * 16, cells)
    red_x[pos] = lax.dot_general(
        left, right, (((1,), (1,)), ((), ())), precision=lax.Precision.HIGHEST, preferred_element_type=F32
    )

    def exchange(array, at, send, recv, peer, count):
        sent = spread(array, at, send, recv, peer, count)
        for s in sent:
            s.start()
        for s in sent:
            s.wait_recv()
        return sent

    def total(array, count):
        value = array[0]
        for i in range(1, count):
            value = value + array[i]
        return value

    begun += exchange(red_x, pos, x_send, x_recv, x_peer, SPAN)
    red_y[where] = total(red_x, SPAN)
    begun += exchange(red_y, where, y_send, y_recv, y_peer, ny)
    whole = total(red_y, ny)
    r_out[...] = whole[16:24]
    red_z[mz] = whole[0:16]
    begun += exchange(red_z, mz, k_send, k_recv, z_peer, nz)
    k_out[...] = red_z[...].reshape(nz * 16, nz * 16)
    for m in range(2):
        for s in to_z(wa, m, 2 * m + 1):
            s.wait_recv()
    v_out[...] = va[...].reshape(nz * 16, cells)
    w_out[...] = wa[...].reshape(nz * 16, cells)
    for s in begun:
        s.wait_send()
    for m in range(2):
        ahead = copy(fsrc.at[m], fdst.at[m], f_send.at[m], f_recv.at[m], (me + 1, mz))
        back = copy(va.at[mz, m], above.at[m], b_send.at[m], b_recv.at[m], (me - 1, mz))
        on = copy(va.at[mz, m], below.at[m], h_send.at[m], h_recv.at[m], (me + 1, mz))

        @pl.when(jnp.logical_not(last))
        def _():
            ahead.wait_send()

        @pl.when(has_before)
        def _():
            back.wait_send()

        @pl.when(has_next)
        def _():
            on.wait_send()


def krylov(nr, nz, r, matrices):
    rhs, cells = r.shape
    ny = nr // SPAN
    dma = pltpu.SemaphoreType.DMA
    every = nz * 2 * rhs
    return pl.pallas_call(
        functools.partial(krylov_kernel, nr, nz),
        out_shape=[
            jax.ShapeDtypeStruct((every, cells), F32),
            jax.ShapeDtypeStruct((every, cells), F32),
            jax.ShapeDtypeStruct((every, every), F32),
            jax.ShapeDtypeStruct((rhs, every), F32),
        ],
        in_specs=[VMEM] * 10,
        out_specs=[VMEM] * 4,
        scratch_shapes=[
            pltpu.VMEM((nz, 2, rhs, cells), F32),
            pltpu.VMEM((nz, 2, rhs, cells), F32),
            pltpu.VMEM((2, rhs, cells), F32),
            pltpu.VMEM((2, rhs, cells), F32),
            pltpu.VMEM((2, rhs, cells), F32),
            pltpu.VMEM((2, rhs, cells), F32),
            pltpu.VMEM((rhs, cells), F32),
            pltpu.VMEM((SPAN, 3 * rhs, every), F32),
            pltpu.VMEM((ny, 3 * rhs, every), F32),
            pltpu.VMEM((nz, 2 * rhs, every), F32),
        ]
        + [dma((2,))] * 6
        + [dma((4, max(nz - 1, 1)))] * 2
        + [dma((SPAN - 1,))] * 2
        + [dma((max(ny - 1, 1),))] * 2
        + [dma((max(nz - 1, 1),))] * 2,
        compiler_params=pltpu.CompilerParams(
            collective_id=0, has_side_effects=True, vmem_limit_bytes=24 * MIB
        ),
    )(r, *matrices)


def solve_kernel(k_in, rt, v, w, r, x_out, r_out):
    size = k_in.shape[0]
    k = 0.5 * (k_in[...] + k_in[...].T)
    row_of = lax.broadcasted_iota(jnp.int32, (size, 1), 0)
    col_of = lax.broadcasted_iota(jnp.int32, (1, size), 1)
    for step in range(size):
        inv = 1.0 / k[step : step + 1, step : step + 1]
        row = jnp.where(col_of == step, 1.0, k[step : step + 1, :]) * inv
        col = jnp.where(row_of == step, -1.0, k[:, step : step + 1])
        k = jnp.where((row_of == step) | (col_of == step), 0.0, k) - col * row
    high = lax.Precision.HIGHEST
    c = jnp.dot(rt[...], k, precision=high, preferred_element_type=F32)
    x_out[...] = jnp.dot(c, v[...], precision=high, preferred_element_type=F32)
    r_out[...] = r[...] - jnp.dot(c, w[...], precision=high, preferred_element_type=F32)


def solve(k, rt, v, w, r):
    return pl.pallas_call(
        solve_kernel,
        out_shape=[jax.ShapeDtypeStruct(r.shape, F32)] * 2,
        in_specs=[VMEM] * 5,
        out_specs=[VMEM] * 2,
        compiler_params=pltpu.CompilerParams(vmem_limit_bytes=16 * MIB),
    )(k, rt, v, w, r)


def solution(mesh):
    nr, nz = mesh.shape["rows"], mesh.shape["rhs"]

    def shards(right_side, tiles, pivots, columns):
        matrices = setup(columns, tiles, pivots)
        v, w, k, rt = krylov(nr, nz, right_side, matrices)
        return tuple(solve(k, rt, v, w, right_side))

    return jax.shard_map(
        shards,
        mesh=mesh,
        in_specs=(
            P("rhs", "rows"),
            P("rows", None, None, None),
            P("rows", None, None),
            P("rows", None),
        ),
        out_specs=(P("rhs", "rows"), P("rhs", "rows")),
        check_vma=False,
    )
```

time: 1240 us -> 108 us (0.09)
  the two profiles are of different devices: /device:TPU:32 before, /device:TPU:4 now
where the time goes in v1:
time: 108 us
  Pallas kernels  104 us (96%)
  local copies, waits for them, and re-layouts  3.13 us (3%)
    pallas_call x1, Pallas kernels, krylov(): pl.pallas_call(functools.partial(krylov_kernel, nr, nz), out_shape=[jax.S...  85.4 us
    pallas_call x1, Pallas kernels, solve(): pl.pallas_call(solve_kernel, out_shape=[jax.ShapeDtypeStruct(r.shape, F32...  12 us
    pallas_call x1, Pallas kernels, setup(): pl.pallas_call(setup_kernel, out_shape=[jax.ShapeDtypeStruct(s, BF) for s...  6.56 us
    unnamed x8, local copies, waits for them, and re-layouts  3.13 us

profile of v1, /device:TPU:4, one launch (start us, length us, event | category | flops | bytes accessed | tf_op | source)
XLA Modules:
  0.0 107.7 jit_solution(6543831193388409423)
XLA Ops:
  0.6 0.0 copy-start
  0.6 1.5 %copy-done = f32[8,7,64,64]{3,2,1,0:T(8,128)S(1)} copy-done((f32[8,7,64,64]{3,2,1,0:T(8,128)S(1)}, f32[8,7,64,64]{3,2,1,0:T(8,128)}, u32[]{:S(2)}) %copy-start) | copy-done | bytes 917528
  2.1 0.0 copy-start.1
  2.1 0.9 copy-done.1
  3.1 0.0 copy-start.3
  3.1 0.7 copy-done.3
  3.8 0.0 copy-start.2
  3.8 6.6 %shard_map.59 = (bf16[1536,512]{1,0:T(8,128)(2,1)S(1)}, bf16[1536,512]{1,0:T(8,128)(2,1)S(1)}, bf16[1536,512]{1,0:T(8,128)(2,1)S(1)}, bf16[512,512]{1,0:T(8,128)...) custom-call(s32[8,7]{1,0:T(8,128)S(1)} %copy-done.3, ...), custom_call_target="tpu_custom_call" | custom-call | tf_op jit(solution)/shard_map/pallas_call | solution.py:118
  10.3 0.0 copy-done.2
  10.4 85.4 %shard_map.60 = (f32[128,512]{1,0:T(8,128)S(1)}, f32[128,512]{1,0:T(8,128)S(1)}, f32[128,128]{1,0:T(8,128)S(1)}, f32[8,128]{1,0:T(8,128)S(1)}) custom-call(f32[8,512]{1,0:T(8,128)S(1)} %copy-done.2, bf16[1536,512]{1,0:T(8,128)(2,1)S(1)} %get-tuple-element.15.dh, bf16[1536,512]{1,0:T(8,128)(2,1)S(1)} %get-tuple-element.16.dm, ...), custom_call_target="tpu_custom_call" | custom-call | tf_op jit(solution)/shard_map/pallas_call | solution.py:332
  95.7 12.0 %shard_map.61 = (f32[8,512]{1,0:T(8,128)}, f32[8,512]{1,0:T(8,128)}) custom-call(f32[128,128]{1,0:T(8,128)S(1)} %get-tuple-element.24.k_in, f32[8,128]{1,0:T(8,128)S(1)} %get-tuple-element.25.rt, f32[128,512]{1,0:T(8,128)S(1)} %get-tuple-element.26.v, f32[128,512]{1,0:T(8,128)S(1)} %get-tuple-element.27.w, f32[8,512]{1,0:T(8,128)S(1)} %copy-done.2), custom_call_target="tpu_custom_call" | custom-call | tf_op jit(solution)/shard_map/pallas_call | solution.py:382
Async XLA Ops:
  0.6 1.5 %copy-start = (f32[8,7,64,64]{3,2,1,0:T(8,128)S(1)}, f32[8,7,64,64]{3,2,1,0:T(8,128)}, u32[]{:S(2)}) copy-start(f32[8,7,64,64]{3,2,1,0:T(8,128)} %tiles.1) | copy-start | bytes 2752516
  2.1 0.9 copy-start.1
  3.1 0.7 copy-start.3
  3.8 6.6 %copy-start.2 = (f32[8,512]{1,0:T(8,128)S(1)}, f32[8,512]{1,0:T(8,128)}, u32[]{:S(2)}) copy-start(f32[8,512]{1,0:T(8,128)} %r.3) | copy-start | bytes 49156

commit v2 on v1

--- a/solution.py
+++ b/solution.py
@@ -48,7 +48,7 @@
     return total
 
 
-def setup_kernel(cols, tiles, pivots, dh, dm, dl, nh, nl, th, tl, sh, sl, dense, pf):
+def setup_kernel(cols, tiles, pivots, dh, dm, dl, nh, nl, th, tl, sh, sl, tf, sf, dense, pf):
     rows, slots, bs = tiles.shape[0], tiles.shape[1], tiles.shape[2]
     cells = rows * bs
     half = cells // 2
@@ -101,13 +101,17 @@
     right = pf[...]
     n = mul(dense[2 * cells : 3 * cells], right)
     nh[...], nl[...] = parts(n, 2)
-    th[...], tl[...] = parts(n.T, 2)
+    nt = n.T
+    tf[...] = nt
+    th[...], tl[...] = parts(nt, 2)
     fxt, fbt = fx.T, fb.T
     low = mul(fbt, right[half:cells])
+    sf[half:cells] = low
     sh[half:cells], sl[half:cells] = parts(low, 2)
     high = mul(fxt, right[half:cells])
     corner = mul(fa.T, right[0:half, 0:half])
     high = jnp.concatenate([high[:, 0:half] + corner, high[:, half:cells]], axis=1)
+    sf[0:half] = high
     sh[0:half], sl[0:half] = parts(high, 2)
 
 
@@ -117,24 +121,34 @@
     shapes = [(3 * cells, cells)] * 3 + [(cells, cells)] * 6
     return pl.pallas_call(
         setup_kernel,
-        out_shape=[jax.ShapeDtypeStruct(s, BF) for s in shapes],
+        out_shape=[jax.ShapeDtypeStruct(s, BF) for s in shapes] + [jax.ShapeDtypeStruct((cells, cells), F32)] * 2,
         in_specs=[SMEM, VMEM, VMEM],
-        out_specs=[VMEM] * 9,
+        out_specs=[VMEM] * 11,
         scratch_shapes=[pltpu.VMEM((3 * cells, cells), F32), pltpu.VMEM((cells, cells), F32)],
         compiler_params=pltpu.CompilerParams(vmem_limit_bytes=40 * MIB),
     )(cols, tiles, pivots)
 
 
+def mul_parts(a, b):
+    (ah, al), (bh, bl) = a, b
+    return dot(ah, bh) + (dot(ah, bl) + dot(al, bh))
+
+
 def krylov_kernel(
     nr, nz,
-    r, dh, dm, dl, nh, nl, th, tl, sh, sl,
+    r, dh, dm, dl, nh, nl, th, tl, sh, sl, tf, sf,
     v_out, w_out, k_out, r_out,
-    va, wa, fsrc, fdst, above, below, c, red_x, red_y, red_z,
-    f_send, f_recv, b_send, b_recv, h_send, h_recv,
+    va, wa, c, sv, other, joint,
+    u_src, u_dst, s_src, s_dst, k_src, k_dst, w_src, w_dst, far, above, below,
+    red_x, red_y, red_z,
+    link_send, link_recv, pair_send, pair_recv,
     z_send, z_recv, x_send, x_recv, y_send, y_recv, k_send, k_recv,
 ):
     me, mz = lax.axis_index("rows"), lax.axis_index("rhs")
     pos, where = lax.rem(me, SPAN), lax.div(me, SPAN)
+    chip, odd = lax.div(pos, 2), lax.rem(pos, 2) == 1
+    even = jnp.logical_not(odd)
+    chips = SPAN // 2
     ny = nr // SPAN
     first, last = pos == 0, pos == SPAN - 1
     cells = r.shape[1]
@@ -159,7 +173,8 @@
         hello(y_peer(o))
     for o in range(1, nz):
         hello(z_peer(o))
-    from_before, to_next = first & (me > 0), last & (me < nr - 1)
+    has_before, has_next = me > 0, me < nr - 1
+    from_before, to_next = first & has_before, last & has_next
 
     @pl.when(from_before)
     def _():
@@ -178,6 +193,21 @@
             device_id=device, device_id_type=pl.DeviceIdType.MESH,
         )
 
+    def link(kind, m, src, dst, device):
+        return copy(src, dst.at[m], link_send.at[kind, m], link_recv.at[kind, m], (device, mz))
+
+    def links(m):
+        z = va.at[mz, m]
+        return dict(
+            u=link(0, m, u_src.at[m], u_dst, me + 1),
+            s=link(1, m, s_src.at[m], s_dst, me - 1),
+            k=link(2, m, k_src.at[m], k_dst, me + 2),
+            w=link(3, m, w_src.at[m], w_dst, me + 1),
+            far=link(4, m, z, far, me - 2),
+            back=link(5, m, z, above, me - 1),
+            on=link(6, m, z, below, me + 1),
+        )
+
     def to_z(array, m, kind):
         return [
             copy(array.at[mz, m], array.at[mz, m], z_send.at[kind, o - 1], z_recv.at[kind, o - 1], z_peer(o))
@@ -190,7 +220,20 @@
         ]
 
     begun = []
-    has_before, has_next = me > 0, me < nr - 1
+
+    def begin(copies):
+        for s in copies:
+            s.start()
+        begun.extend(copies)
+
+    pair = [
+        copy(ref, other.at[i], pair_send.at[i], pair_recv.at[i], (me - 1, mz)) for i, ref in enumerate((tf, sf))
+    ]
+
+    @pl.when(odd)
+    def _():
+        for p in pair:
+            p.start()
 
     @pl.when(me == 0)
     def _():
@@ -199,91 +242,183 @@
     @pl.when(me == nr - 1)
     def _():
         above[...] = jnp.zeros(above.shape, F32)
-
-    n_parts, t_parts, s_parts = (nh, nl), (th, tl), (sh, sl)
 
     def values(refs, rows=slice(None)):
         return [ref[rows] for ref in refs]
 
+    n_refs, t_refs, s_refs = (nh, nl), (th, tl), (sh, sl)
+    kt_refs, k_refs, e_refs = ((joint.at[2 * i], joint.at[2 * i + 1]) for i in range(3))
+
+    def product_of_two():
+        pair[0].wait_recv()
+        kt = mul_parts(values(t_refs), parts(other[0], 2))
+        for ref, p in zip(kt_refs, parts(kt, 2)):
+            ref[...] = p
+        return kt
+
+    def middle_of_two():
+        pair[1].wait_recv()
+        x = mul_parts(parts(other[1], 2), values(n_refs))
+        e = sf[...] + mul_parts(values(t_refs), parts(x, 2))
+        for ref, p in zip(e_refs, parts(e, 2)):
+            ref[...] = p
+        k = (kt_refs[0][...].astype(F32) + kt_refs[1][...].astype(F32)).T
+        for ref, p in zip(k_refs, parts(k, 2)):
+            ref[...] = p
+
+    @pl.when(even)
+    def _():
+        product_of_two()
+
     for m in range(2):
         source = r if m == 0 else wa.at[mz, 0]
-        ahead = copy(fsrc.at[m], fdst.at[m], f_send.at[m], f_recv.at[m], (me + 1, mz))
-        back = copy(va.at[mz, m], above.at[m], b_send.at[m], b_recv.at[m], (me - 1, mz))
-        on = copy(va.at[mz, m], below.at[m], h_send.at[m], h_recv.at[m], (me + 1, mz))
+        at = links(m)
+
+        def prepare():
+            if m == 0:
+                middle_of_two()
+            at["s"].wait_recv()
+            sv[...] = times(s_dst[m], values(n_refs))
+
+        @pl.when(odd & (chip < chips - 1))
+        def _():
+            u_src[m] = times(source[...], values(t_refs))
+            at["u"].start()
+
+        @pl.when(odd)
+        def _():
+            s_src[m] = times(source[...], values(s_refs))
+            at["s"].start()
+            at["w"].wait_recv()
+            c[...] = times(source[...] - w_dst[m], values(s_refs))
+
+        @pl.when(odd & (chip < chips - 1))
+        def _():
+            at["back"].wait_recv()
+            va[mz, m] = c[...] - times(above[m], values(n_refs))
+
+        @pl.when(last)
+        def _():
+            va[mz, m] = c[...]
 
         @pl.when(first)
         def _():
             c[...] = source[...]
 
+        @pl.when(even & (chip > 0))
+        def _():
+            prepare()
+            at["u"].wait_recv()
+            at["k"].wait_recv()
+            c[...] = source[...] - u_dst[m] + k_dst[m]
+
+        @pl.when(even & (chip < chips - 1))
+        def _():
+            k_src[m] = times(c[...], values(kt_refs))
+            at["k"].start()
+
+        @pl.when(even)
+        def _():
+            w_src[m] = times(c[...], values(t_refs))
+            at["w"].start()
+
+        @pl.when(first)
+        def _():
+            prepare()
+
+        @pl.when(even)
+        def _():
+            c[...] = times(c[...], values(e_refs)) - sv[...]
+
+        @pl.when(even & (chip < chips - 1))
+        def _():
+            at["far"].wait_recv()
+            va[mz, m] = c[...] + times(far[m], values(k_refs))
+
+        @pl.when(even & (chip == chips - 1))
+        def _():
+            va[mz, m] = c[...]
+
+        @pl.when(even & (chip > 0))
+        def _():
+            at["far"].start()
+
+        @pl.when(has_before)
+        def _():
+            at["back"].start()
+
+        @pl.when(has_next)
+        def _():
+            at["on"].start()
+
+        begin(to_z(va, m, 2 * m))
+
+        d = (dh, dm, dl)
+
+        def part(value, i):
+            return times(value, values(d, slice(i * cells, (i + 1) * cells)))
+
+        c[...] = part(va[mz, m], 1)
+
+        @pl.when(from_before)
+        def _():
+            at["on"].wait_recv()
+
+        @pl.when(first)
+        def _():
+            wa[mz, m] = part(below[m], 0)
+
+        @pl.when(jnp.logical_not(odd) )
+        def _():
+            at["back"].wait_recv()
+
+        @pl.when(jnp.logical_not(last))
+        def _():
+            sv[...] = part(above[m], 2)
+
+        if m == 1:
+            @pl.when(first)
+            def _():
+                far[0] = 0.5 * c[...] + sv[...] + wa[mz, m]
+
+            @pl.when(jnp.logical_not(first | last))
+            def _():
+                far[0] = 0.5 * c[...] + sv[...]
+
+            @pl.when(last)
+            def _():
+                far[0] = 0.5 * c[...]
+
+            for kind in range(2):
+                for s in to_z(va, kind, 2 * kind):
+                    s.wait_recv()
+            left = jnp.concatenate([wa[mz, 0], far[0], r[...]], axis=0)
+            right = va[...].reshape(nz * 16, cells)
+            red_x[pos] = lax.dot_general(
+                left, right, (((1,), (1,)), ((), ())),
+                precision=lax.Precision.HIGHEST, preferred_element_type=F32,
+            )
+            over_x = spread(red_x, pos, x_send, x_recv, x_peer, SPAN)
+            begin(over_x)
+
+        @pl.when(to_next)
+        def _():
+            at["back"].wait_recv()
+
+        @pl.when(last)
+        def _():
+            sv[...] = part(above[m], 2)
+
+        @pl.when(has_before & jnp.logical_not(first))
+        def _():
+            at["on"].wait_recv()
+
         @pl.when(jnp.logical_not(first))
         def _():
-            ahead.wait_recv()
-            c[...] = source[...] - fdst[m]
-
-        @pl.when(jnp.logical_not(last))
-        def _():
-            fsrc[m] = times(c[...], values(t_parts))
-            ahead.start()
-
-        c[...] = times(c[...], values(s_parts))
-
-        @pl.when(last)
-        def _():
-            va[mz, m] = c[...]
-
-        @pl.when(jnp.logical_not(last))
-        def _():
-            back.wait_recv()
-            va[mz, m] = c[...] - times(above[m], values(n_parts))
-
-        @pl.when(has_before)
-        def _():
-            back.start()
-
-        @pl.when(has_next)
-        def _():
-            on.start()
-
-        sent = to_z(va, m, 2 * m)
-        for s in sent:
-            s.start()
-        begun += sent
-
-        d = (dh, dm, dl)
-        q = times(va[mz, m], values(d, slice(cells, 2 * cells)))
-
-        @pl.when(to_next)
-        def _():
-            back.wait_recv()
-
-        q = q + times(above[m], values(d, slice(2 * cells, 3 * cells)))
-
-        @pl.when(has_before)
-        def _():
-            on.wait_recv()
-
-        wa[mz, m] = q + times(below[m], values(d, slice(0, cells)))
-        sent = to_z(wa, m, 2 * m + 1)
-        for s in sent:
-            s.start()
-        begun += sent
-
-    for m in range(2):
-        for s in to_z(va, m, 2 * m):
-            s.wait_recv()
-    left = jnp.concatenate([wa[mz, 0], wa[mz, 1], r[...]], axis=0)
-    right = va[...].reshape(nz * 16, cells)
-    red_x[pos] = lax.dot_general(
-        left, right, (((1,), (1,)), ((), ())), precision=lax.Precision.HIGHEST, preferred_element_type=F32
-    )
-
-    def exchange(array, at, send, recv, peer, count):
-        sent = spread(array, at, send, recv, peer, count)
-        for s in sent:
-            s.start()
-        for s in sent:
-            s.wait_recv()
-        return sent
+            wa[mz, m] = part(below[m], 0)
+
+        wa[mz, m] = c[...] + sv[...] + wa[mz, m]
+        begin(to_z(wa, m, 2 * m + 1))
 
     def total(array, count):
         value = array[0]
@@ -291,37 +426,49 @@
             value = value + array[i]
         return value
 
-    begun += exchange(red_x, pos, x_send, x_recv, x_peer, SPAN)
+    for s in over_x:
+        s.wait_recv()
     red_y[where] = total(red_x, SPAN)
-    begun += exchange(red_y, where, y_send, y_recv, y_peer, ny)
+    over_y = spread(red_y, where, y_send, y_recv, y_peer, ny)
+    begin(over_y)
+    for s in over_y:
+        s.wait_recv()
     whole = total(red_y, ny)
     r_out[...] = whole[16:24]
     red_z[mz] = whole[0:16]
-    begun += exchange(red_z, mz, k_send, k_recv, z_peer, nz)
-    k_out[...] = red_z[...].reshape(nz * 16, nz * 16)
+    over_z = spread(red_z, mz, k_send, k_recv, z_peer, nz)
+    begin(over_z)
     for m in range(2):
         for s in to_z(wa, m, 2 * m + 1):
             s.wait_recv()
     v_out[...] = va[...].reshape(nz * 16, cells)
     w_out[...] = wa[...].reshape(nz * 16, cells)
+    for s in over_z:
+        s.wait_recv()
+    k_out[...] = red_z[...].reshape(nz * 16, nz * 16)
     for s in begun:
         s.wait_send()
+
+    @pl.when(odd)
+    def _():
+        for p in pair:
+            p.wait_send()
+
     for m in range(2):
-        ahead = copy(fsrc.at[m], fdst.at[m], f_send.at[m], f_recv.at[m], (me + 1, mz))
-        back = copy(va.at[mz, m], above.at[m], b_send.at[m], b_recv.at[m], (me - 1, mz))
-        on = copy(va.at[mz, m], below.at[m], h_send.at[m], h_recv.at[m], (me + 1, mz))
-
-        @pl.when(jnp.logical_not(last))
-        def _():
-            ahead.wait_send()
-
-        @pl.when(has_before)
-        def _():
-            back.wait_send()
-
-        @pl.when(has_next)
-        def _():
-            on.wait_send()
+        at = links(m)
+        for name, started in (
+            ("u", odd & (chip < chips - 1)),
+            ("s", odd),
+            ("k", even & (chip < chips - 1)),
+            ("w", even),
+            ("far", even & (chip > 0)),
+            ("back", has_before),
+            ("on", has_next),
+        ):
+
+            @pl.when(started)
+            def _():
+                at[name].wait_send()
 
 
 def krylov(nr, nz, r, matrices):
@@ -329,6 +476,8 @@
     ny = nr // SPAN
     dma = pltpu.SemaphoreType.DMA
     every = nz * 2 * rhs
+    vector = pltpu.VMEM((rhs, cells), F32)
+    vectors = pltpu.VMEM((2, rhs, cells), F32)
     return pl.pallas_call(
         functools.partial(krylov_kernel, nr, nz),
         out_shape=[
@@ -337,41 +486,49 @@
             jax.ShapeDtypeStruct((every, every), F32),
             jax.ShapeDtypeStruct((rhs, every), F32),
         ],
-        in_specs=[VMEM] * 10,
+        in_specs=[VMEM] * 12,
         out_specs=[VMEM] * 4,
-        scratch_shapes=[
-            pltpu.VMEM((nz, 2, rhs, cells), F32),
-            pltpu.VMEM((nz, 2, rhs, cells), F32),
-            pltpu.VMEM((2, rhs, cells), F32),
-            pltpu.VMEM((2, rhs, cells), F32),
-            pltpu.VMEM((2, rhs, cells), F32),
-            pltpu.VMEM((2, rhs, cells), F32),
-            pltpu.VMEM((rhs, cells), F32),
+        scratch_shapes=[pltpu.VMEM((nz, 2, rhs, cells), F32)] * 2
+        + [vector] * 2
+        + [pltpu.VMEM((2, cells, cells), F32), pltpu.VMEM((6, cells, cells), BF)]
+        + [vectors] * 11
+        + [
             pltpu.VMEM((SPAN, 3 * rhs, every), F32),
             pltpu.VMEM((ny, 3 * rhs, every), F32),
             pltpu.VMEM((nz, 2 * rhs, every), F32),
         ]
-        + [dma((2,))] * 6
+        + [dma((7, 2))] * 2
+        + [dma((2,))] * 2
         + [dma((4, max(nz - 1, 1)))] * 2
         + [dma((SPAN - 1,))] * 2
         + [dma((max(ny - 1, 1),))] * 2
         + [dma((max(nz - 1, 1),))] * 2,
         compiler_params=pltpu.CompilerParams(
-            collective_id=0, has_side_effects=True, vmem_limit_bytes=24 * MIB
+            collective_id=0, has_side_effects=True, vmem_limit_bytes=32 * MIB
         ),
     )(r, *matrices)
 
 
 def solve_kernel(k_in, rt, v, w, r, x_out, r_out):
     size = k_in.shape[0]
-    k = 0.5 * (k_in[...] + k_in[...].T)
+    k = k_in[...]
+    kt = k.T
     row_of = lax.broadcasted_iota(jnp.int32, (size, 1), 0)
     col_of = lax.broadcasted_iota(jnp.int32, (1, size), 1)
-    for step in range(size):
-        inv = 1.0 / k[step : step + 1, step : step + 1]
-        row = jnp.where(col_of == step, 1.0, k[step : step + 1, :]) * inv
-        col = jnp.where(row_of == step, -1.0, k[:, step : step + 1])
-        k = jnp.where((row_of == step) | (col_of == step), 0.0, k) - col * row
+    row_p, col_p = lax.rem(row_of // 8, 2) == 1, lax.rem(col_of // 8, 2) == 1
+    both = k + kt
+    k = jnp.where(row_p, jnp.where(col_p, both, kt), jnp.where(col_p, k, 0.5 * both))
+    for i in range(0, size, 2):
+        j = i + 1
+        a, b, d = k[i : i + 1, i : i + 1], k[i : i + 1, j : j + 1], k[j : j + 1, j : j + 1]
+        inv = 1.0 / (a * d - b * b)
+        ra = jnp.where(col_of == i, 1.0, jnp.where(col_of == j, 0.0, k[i : i + 1, :]))
+        rb = jnp.where(col_of == j, 1.0, jnp.where(col_of == i, 0.0, k[j : j + 1, :]))
+        new_a, new_b = (d * ra - b * rb) * inv, (a * rb - b * ra) * inv
+        ca = jnp.where(row_of == i, -1.0, jnp.where(row_of == j, 0.0, k[:, i : i + 1]))
+        cb = jnp.where(row_of == j, -1.0, jnp.where(row_of == i, 0.0, k[:, j : j + 1]))
+        gone = (row_of == i) | (row_of == j) | (col_of == i) | (col_of == j)
+        k = jnp.where(gone, 0.0, k) - ca * new_a - cb * new_b
     high = lax.Precision.HIGHEST
     c = jnp.dot(rt[...], k, precision=high, preferred_element_type=F32)
     x_out[...] = jnp.dot(c, v[...], precision=high, preferred_element_type=F32)

time: 108 us -> 99 us (0.917)
  Pallas kernels: 104 us -> 95 us
    pallas_call x1, Pallas kernels: 85.4 us -> 75.9 us  [krylov(): pl.pallas_call(functools.partial(krylov_kernel, nr, nz), out_shape=[jax.S...]
where the time goes in v2:
time: 99 us; the launch traced here: 98.7 us
  Pallas kernels  95 us (96%)
  local copies, waits for them, and re-layouts  3.13 us (3%)
    pallas_call x1, Pallas kernels, krylov(): pl.pallas_call(functools.partial(krylov_kernel, nr, nz), out_shape=[jax.S...  75.9 us
    pallas_call x1, Pallas kernels, solve(): pl.pallas_call(solve_kernel, out_shape=[jax.ShapeDtypeStruct(r.shape, F32...  12.4 us
    pallas_call x1, Pallas kernels, setup(): pl.pallas_call(setup_kernel, out_shape=[jax.ShapeDtypeStruct(s, BF) for s...  6.61 us
    unnamed x8, local copies, waits for them, and re-layouts  3.13 us

profile of v2, /device:TPU:4, one launch (start us, length us, event | category | flops | bytes accessed | tf_op | source)
XLA Modules:
  0.0 98.7 jit_solution(13079851021387381480)
XLA Ops:
  0.6 0.0 copy-start
  0.6 1.5 %copy-done = f32[8,7,64,64]{3,2,1,0:T(8,128)S(1)} copy-done((f32[8,7,64,64]{3,2,1,0:T(8,128)S(1)}, f32[8,7,64,64]{3,2,1,0:T(8,128)}, u32[]{:S(2)}) %copy-start) | copy-done | bytes 917528
  2.1 0.0 copy-start.1
  2.1 0.9 copy-done.1
  3.1 0.0 copy-start.3
  3.1 0.7 copy-done.3
  3.8 0.0 copy-start.2
  3.8 6.6 %shard_map.59 = (bf16[1536,512]{1,0:T(8,128)(2,1)S(1)}, bf16[1536,512]{1,0:T(8,128)(2,1)S(1)}, bf16[1536,512]{1,0:T(8,128)(2,1)S(1)}, bf16[512,512]{1,0:T(8,128)...) custom-call(s32[8,7]{1,0:T(8,128)S(1)} %copy-done.3, ...), custom_call_target="tpu_custom_call" | custom-call | tf_op jit(solution)/shard_map/pallas_call | solution.py:122
  10.4 0.0 copy-done.2
  10.4 75.9 %shard_map.60 = (f32[128,512]{1,0:T(8,128)S(1)}, f32[128,512]{1,0:T(8,128)S(1)}, f32[128,128]{1,0:T(8,128)S(1)}, f32[8,128]{1,0:T(8,128)S(1)}) custom-call(f32[8,512]{1,0:T(8,128)S(1)} %copy-done.2, bf16[1536,512]{1,0:T(8,128)(2,1)S(1)} %get-tuple-element.17.dh, bf16[1536,512]{1,0:T(8,128)(2,1)S(1)} %get-tuple-element.18.dm, ...), custom_call_target="tpu_custom_call" | custom-call | tf_op jit(solution)/shard_map/pallas_call | solution.py:481
  86.3 12.4 %shard_map.61 = (f32[8,512]{1,0:T(8,128)}, f32[8,512]{1,0:T(8,128)}) custom-call(f32[128,128]{1,0:T(8,128)S(1)} %get-tuple-element.28.k_in, f32[8,128]{1,0:T(8,128)S(1)} %get-tuple-element.29.rt, f32[128,512]{1,0:T(8,128)S(1)} %get-tuple-element.30.v, f32[128,512]{1,0:T(8,128)S(1)} %get-tuple-element.31.w, f32[8,512]{1,0:T(8,128)S(1)} %copy-done.2), custom_call_target="tpu_custom_call" | custom-call | tf_op jit(solution)/shard_map/pallas_call | solution.py:539
Async XLA Ops:
  0.6 1.5 %copy-start = (f32[8,7,64,64]{3,2,1,0:T(8,128)S(1)}, f32[8,7,64,64]{3,2,1,0:T(8,128)}, u32[]{:S(2)}) copy-start(f32[8,7,64,64]{3,2,1,0:T(8,128)} %tiles.1) | copy-start | bytes 2752516
  2.1 0.9 copy-start.1
  3.1 0.7 copy-start.3
  3.8 6.6 %copy-start.2 = (f32[8,512]{1,0:T(8,128)S(1)}, f32[8,512]{1,0:T(8,128)}, u32[]{:S(2)}) copy-start(f32[8,512]{1,0:T(8,128)} %r.3) | copy-start | bytes 49156

commit v3 on v2

--- a/solution.py
+++ b/solution.py
@@ -48,85 +48,32 @@
     return total
 
 
-def setup_kernel(cols, tiles, pivots, dh, dm, dl, nh, nl, th, tl, sh, sl, tf, sf, dense, pf):
-    rows, slots, bs = tiles.shape[0], tiles.shape[1], tiles.shape[2]
-    cells = rows * bs
-    half = cells // 2
+def assemble_kernel(cols, tiles, dense, held, sems):
+    rows, slots, bs = held.shape[0], held.shape[1], held.shape[2]
     start = lax.axis_index("rows") * rows
+    copies = [pltpu.make_async_copy(tiles.at[i], held.at[i], sems.at[i]) for i in range(rows)]
+    for c in copies:
+        c.start()
     dense[...] = jnp.zeros(dense.shape, F32)
     for i in range(rows):
+        copies[i].wait()
         for k in range(slots):
             j = cols[i, k] - start + rows
             at = (pl.ds(pl.multiple_of(j * bs, bs), bs), slice(i * bs, (i + 1) * bs))
-            dense[at] = dense[at] + tiles[i, k].T
-    for at in range(3):
-        part = slice(at * cells, (at + 1) * cells)
-        for ref, p in zip((dh, dm, dl), parts(dense[part], 3)):
-            ref[part] = p
-
-    def block_diagonal(first):
-        zero = jnp.zeros((bs, bs), F32)
-        count = half // bs
-        return jnp.concatenate(
-            [
-                jnp.concatenate([pivots[first + i] if i == j else zero for j in range(count)], axis=1)
-                for i in range(count)
-            ],
-            axis=0,
-        )
-
-    pa, pb = block_diagonal(0), block_diagonal(rows // 2)
-    row = lax.broadcasted_iota(jnp.int32, (half, half), 0)
-    col = lax.broadcasted_iota(jnp.int32, (half, half), 1)
-    same_pair = row // (2 * bs) == col // (2 * bs)
-    eye = (row == col).astype(F32)
-    lower = row // bs > col // bs
-
-    def inverse(block):
-        first = jnp.where(same_pair, block, 0.0)
-        rest = block - first
-        f = eye - first
-        return f - mul(mul(f, rest), f)
-
-    o = cells
-    ga = mul(jnp.where(lower, dense[o : o + half, 0:half], 0.0), pa)
-    gb = mul(jnp.where(lower, dense[o + half : o + cells, half:cells], 0.0), pb)
-    gx = mul(dense[o + half : o + cells, 0:half], pa)
-    fa, fb = inverse(ga), inverse(gb)
-    fx = -mul(mul(fb, gx), fa)
-    pf[0:half, 0:half] = mul(pa, fa)
-    pf[0:half, half:cells] = jnp.zeros((half, half), F32)
-    pf[half:cells, 0:half] = mul(pb, fx)
-    pf[half:cells, half:cells] = mul(pb, fb)
-    right = pf[...]
-    n = mul(dense[2 * cells : 3 * cells], right)
-    nh[...], nl[...] = parts(n, 2)
-    nt = n.T
-    tf[...] = nt
-    th[...], tl[...] = parts(nt, 2)
-    fxt, fbt = fx.T, fb.T
-    low = mul(fbt, right[half:cells])
-    sf[half:cells] = low
-    sh[half:cells], sl[half:cells] = parts(low, 2)
-    high = mul(fxt, right[half:cells])
-    corner = mul(fa.T, right[0:half, 0:half])
-    high = jnp.concatenate([high[:, 0:half] + corner, high[:, half:cells]], axis=1)
-    sf[0:half] = high
-    sh[0:half], sl[0:half] = parts(high, 2)
-
-
-def setup(cols, tiles, pivots):
+            dense[at] = dense[at] + held[i, k].T
+
+
+def assemble(cols, tiles):
     rows, _, bs, _ = tiles.shape
     cells = rows * bs
-    shapes = [(3 * cells, cells)] * 3 + [(cells, cells)] * 6
     return pl.pallas_call(
-        setup_kernel,
-        out_shape=[jax.ShapeDtypeStruct(s, BF) for s in shapes] + [jax.ShapeDtypeStruct((cells, cells), F32)] * 2,
-        in_specs=[SMEM, VMEM, VMEM],
-        out_specs=[VMEM] * 11,
-        scratch_shapes=[pltpu.VMEM((3 * cells, cells), F32), pltpu.VMEM((cells, cells), F32)],
-        compiler_params=pltpu.CompilerParams(vmem_limit_bytes=40 * MIB),
-    )(cols, tiles, pivots)
+        assemble_kernel,
+        out_shape=jax.ShapeDtypeStruct((3 * cells, cells), F32),
+        in_specs=[SMEM, pl.BlockSpec(memory_space=pltpu.HBM)],
+        out_specs=VMEM,
+        scratch_shapes=[pltpu.VMEM(tiles.shape, F32), pltpu.SemaphoreType.DMA((rows,))],
+        compiler_params=pltpu.CompilerParams(vmem_limit_bytes=16 * MIB),
+    )(cols, tiles)
 
 
 def mul_parts(a, b):
@@ -136,8 +83,9 @@
 
 def krylov_kernel(
     nr, nz,
-    r, dh, dm, dl, nh, nl, th, tl, sh, sl, tf, sf,
+    r, dense, pivots,
     v_out, w_out, k_out, r_out,
+    dh, dm, dl, nh, nl, th, tl, sh, sl, tf, sf, pf,
     va, wa, c, sv, other, joint,
     u_src, u_dst, s_src, s_dst, k_src, k_dst, w_src, w_dst, far, above, below,
     red_x, red_y, red_z,
@@ -184,6 +132,48 @@
     def _():
         hello((me + 1, mz))
 
+    bs = pivots.shape[1]
+    half = cells // 2
+
+    def block_diagonal(first_row):
+        zero = jnp.zeros((bs, bs), F32)
+        count = half // bs
+        return jnp.concatenate(
+            [
+                jnp.concatenate([pivots[first_row + i] if i == j else zero for j in range(count)], axis=1)
+                for i in range(count)
+            ],
+            axis=0,
+        )
+
+    pa, pb = block_diagonal(0), block_diagonal(half // bs)
+    row = lax.broadcasted_iota(jnp.int32, (half, half), 0)
+    col = lax.broadcasted_iota(jnp.int32, (half, half), 1)
+    same_pair = row // (2 * bs) == col // (2 * bs)
+    eye = (row == col).astype(F32)
+    lower = row // bs > col // bs
+
+    def inverse(block):
+        within = jnp.where(same_pair, block, 0.0)
+        f = eye - within
+        return f - mul(mul(f, block - within), f)
+
+    o = cells
+    ga = mul(jnp.where(lower, dense[o : o + half, 0:half], 0.0), pa)
+    gb = mul(jnp.where(lower, dense[o + half : o + cells, half:cells], 0.0), pb)
+    gx = mul(dense[o + half : o + cells, 0:half], pa)
+    fa, fb = inverse(ga), inverse(gb)
+    fx = -mul(mul(fb, gx), fa)
+    pf[0:half, 0:half] = mul(pa, fa)
+    pf[0:half, half:cells] = jnp.zeros((half, half), F32)
+    pf[half:cells, 0:half] = mul(pb, fx)
+    pf[half:cells, half:cells] = mul(pb, fb)
+    n = mul(dense[2 * cells : 3 * cells], pf[...])
+    nh[...], nl[...] = parts(n, 2)
+    nt = n.T
+    tf[...] = nt
+    th[...], tl[...] = parts(nt, 2)
+
     edges = from_before.astype(jnp.int32) + to_next.astype(jnp.int32)
     pl.semaphore_wait(barrier, SPAN - 1 + ny - 1 + nz - 1 + edges)
 
@@ -226,14 +216,27 @@
             s.start()
         begun.extend(copies)
 
-    pair = [
-        copy(ref, other.at[i], pair_send.at[i], pair_recv.at[i], (me - 1, mz)) for i, ref in enumerate((tf, sf))
-    ]
-
-    @pl.when(odd)
-    def _():
-        for p in pair:
-            p.start()
+    turn = chip == chips - 1
+    ahead = chip < chips - 1
+    pair_n = copy(tf, other, pair_send.at[0], pair_recv.at[0], (me - 1, mz))
+    pair_s = copy(sf, other, pair_send.at[1], pair_recv.at[1], (me - 1, mz))
+
+    @pl.when(odd & ahead)
+    def _():
+        pair_n.start()
+
+    low = mul(fb.T, pf[half:cells])
+    sf[half:cells] = low
+    sh[half:cells], sl[half:cells] = parts(low, 2)
+    high = mul(fx.T, pf[half:cells])
+    corner = mul(fa.T, pf[0:half, 0:half])
+    high = jnp.concatenate([high[:, 0:half] + corner, high[:, half:cells]], axis=1)
+    sf[0:half] = high
+    sh[0:half], sl[0:half] = parts(high, 2)
+
+    @pl.when(last)
+    def _():
+        pair_s.start()
 
     @pl.when(me == 0)
     def _():
@@ -247,101 +250,146 @@
         return [ref[rows] for ref in refs]
 
     n_refs, t_refs, s_refs = (nh, nl), (th, tl), (sh, sl)
-    kt_refs, k_refs, e_refs = ((joint.at[2 * i], joint.at[2 * i + 1]) for i in range(3))
-
-    def product_of_two():
-        pair[0].wait_recv()
-        kt = mul_parts(values(t_refs), parts(other[0], 2))
+    kt_refs, k_refs = (joint.at[0], joint.at[1]), (joint.at[2], joint.at[3])
+
+    def split_dense():
+        for i in range(3):
+            rows = slice(i * cells, (i + 1) * cells)
+            for ref, p in zip((dh, dm, dl), parts(dense[rows], 3)):
+                ref[rows] = p
+
+    @pl.when(even & ahead)
+    def _():
+        pair_n.wait_recv()
+        kt = mul_parts(values(t_refs), parts(other[...], 2))
         for ref, p in zip(kt_refs, parts(kt, 2)):
             ref[...] = p
-        return kt
-
-    def middle_of_two():
-        pair[1].wait_recv()
-        x = mul_parts(parts(other[1], 2), values(n_refs))
+        other[...] = kt
+
+    @pl.when(even & turn)
+    def _():
+        pair_s.wait_recv()
+        x = mul_parts(parts(other[...], 2), values(n_refs))
         e = sf[...] + mul_parts(values(t_refs), parts(x, 2))
-        for ref, p in zip(e_refs, parts(e, 2)):
+        for ref, p in zip(s_refs, parts(e, 2)):
             ref[...] = p
-        k = (kt_refs[0][...].astype(F32) + kt_refs[1][...].astype(F32)).T
-        for ref, p in zip(k_refs, parts(k, 2)):
+
+    def back_product():
+        for ref, p in zip(k_refs, parts(other[...].T, 2)):
             ref[...] = p
-
-    @pl.when(even)
-    def _():
-        product_of_two()
 
     for m in range(2):
         source = r if m == 0 else wa.at[mz, 0]
         at = links(m)
-
-        def prepare():
-            if m == 0:
-                middle_of_two()
+        begins = 1 if m == 0 else 0
+
+        @pl.when(odd & ahead & (chip >= begins))
+        def _():
+            u_src[m] = times(source[...], values(t_refs))
+            at["u"].start()
+
+        @pl.when(last)
+        def _():
+            s_src[m] = times(source[...], values(s_refs))
+            at["s"].start()
+
+        if m == 0:
+
+            @pl.when(jnp.logical_not(first) & (pos != 1))
+            def _():
+                split_dense()
+
+        @pl.when(odd)
+        def _():
+            at["w"].wait_recv()
+            c[...] = source[...] - w_dst[m]
+
+        @pl.when(odd & (chip < begins))
+        def _():
+            u_src[m] = times(c[...], values(t_refs))
+            at["u"].start()
+
+        @pl.when(odd & ahead)
+        def _():
+            s_src[m] = times(c[...], values(s_refs))
+            at["s"].start()
+
+        if m == 0:
+
+            @pl.when(pos == 1)
+            def _():
+                split_dense()
+
+        @pl.when(odd & ahead)
+        def _():
+            at["back"].wait_recv()
+            va[mz, m] = s_src[m] - times(above[m], values(n_refs))
+
+        @pl.when(last)
+        def _():
+            va[mz, m] = times(c[...], values(s_refs))
+
+        @pl.when(first)
+        def _():
+            c[...] = source[...]
+
+        def other_half():
             at["s"].wait_recv()
             sv[...] = times(s_dst[m], values(n_refs))
 
-        @pl.when(odd & (chip < chips - 1))
-        def _():
-            u_src[m] = times(source[...], values(t_refs))
-            at["u"].start()
-
-        @pl.when(odd)
-        def _():
-            s_src[m] = times(source[...], values(s_refs))
-            at["s"].start()
-            at["w"].wait_recv()
-            c[...] = times(source[...] - w_dst[m], values(s_refs))
-
-        @pl.when(odd & (chip < chips - 1))
-        def _():
-            at["back"].wait_recv()
-            va[mz, m] = c[...] - times(above[m], values(n_refs))
-
-        @pl.when(last)
-        def _():
-            va[mz, m] = c[...]
-
-        @pl.when(first)
-        def _():
-            c[...] = source[...]
+        @pl.when(even & turn)
+        def _():
+            other_half()
 
         @pl.when(even & (chip > 0))
         def _():
-            prepare()
             at["u"].wait_recv()
+            c[...] = source[...] - u_dst[m]
+
+        @pl.when(even & (chip > begins))
+        def _():
             at["k"].wait_recv()
-            c[...] = source[...] - u_dst[m] + k_dst[m]
-
-        @pl.when(even & (chip < chips - 1))
+            c[...] = c[...] + k_dst[m]
+
+        @pl.when(even & ahead & (chip >= begins))
         def _():
             k_src[m] = times(c[...], values(kt_refs))
             at["k"].start()
 
-        @pl.when(even)
+        @pl.when(even & ahead)
         def _():
             w_src[m] = times(c[...], values(t_refs))
             at["w"].start()
 
-        @pl.when(first)
-        def _():
-            prepare()
-
-        @pl.when(even)
-        def _():
-            c[...] = times(c[...], values(e_refs)) - sv[...]
-
-        @pl.when(even & (chip < chips - 1))
-        def _():
+        if m == 0:
+
+            @pl.when(even & ahead)
+            def _():
+                back_product()
+
+            @pl.when(first)
+            def _():
+                split_dense()
+
+        @pl.when(even & ahead)
+        def _():
+            other_half()
+            c[...] = times(c[...], values(s_refs)) - sv[...]
             at["far"].wait_recv()
             va[mz, m] = c[...] + times(far[m], values(k_refs))
 
-        @pl.when(even & (chip == chips - 1))
-        def _():
-            va[mz, m] = c[...]
+        @pl.when(even & turn)
+        def _():
+            va[mz, m] = times(c[...], values(s_refs)) - sv[...]
 
         @pl.when(even & (chip > 0))
         def _():
             at["far"].start()
+
+        @pl.when(even & turn)
+        def _():
+            w_src[m] = times(c[...], values(t_refs))
+            at["w"].start()
 
         @pl.when(has_before)
         def _():
@@ -449,17 +497,20 @@
     for s in begun:
         s.wait_send()
 
-    @pl.when(odd)
-    def _():
-        for p in pair:
-            p.wait_send()
+    @pl.when(odd & ahead)
+    def _():
+        pair_n.wait_send()
+
+    @pl.when(last)
+    def _():
+        pair_s.wait_send()
 
     for m in range(2):
         at = links(m)
         for name, started in (
-            ("u", odd & (chip < chips - 1)),
+            ("u", odd & ahead),
             ("s", odd),
-            ("k", even & (chip < chips - 1)),
+            ("k", even & ahead & (chip >= (1 if m == 0 else 0))),
             ("w", even),
             ("far", even & (chip > 0)),
             ("back", has_before),
@@ -471,12 +522,13 @@
                 at[name].wait_send()
 
 
-def krylov(nr, nz, r, matrices):
+def krylov(nr, nz, r, dense, pivots):
     rhs, cells = r.shape
     ny = nr // SPAN
     dma = pltpu.SemaphoreType.DMA
     every = nz * 2 * rhs
     vector = pltpu.VMEM((rhs, cells), F32)
+    square, square_half = pltpu.VMEM((cells, cells), F32), pltpu.VMEM((cells, cells), BF)
     vectors = pltpu.VMEM((2, rhs, cells), F32)
     return pl.pallas_call(
         functools.partial(krylov_kernel, nr, nz),
@@ -486,11 +538,14 @@
             jax.ShapeDtypeStruct((every, every), F32),
             jax.ShapeDtypeStruct((rhs, every), F32),
         ],
-        in_specs=[VMEM] * 12,
+        in_specs=[VMEM] * 3,
         out_specs=[VMEM] * 4,
-        scratch_shapes=[pltpu.VMEM((nz, 2, rhs, cells), F32)] * 2
+        scratch_shapes=[pltpu.VMEM((3 * cells, cells), BF)] * 3
+        + [square_half] * 6
+        + [square] * 3
+        + [pltpu.VMEM((nz, 2, rhs, cells), F32)] * 2
         + [vector] * 2
-        + [pltpu.VMEM((2, cells, cells), F32), pltpu.VMEM((6, cells, cells), BF)]
+        + [square, pltpu.VMEM((4, cells, cells), BF)]
         + [vectors] * 11
         + [
             pltpu.VMEM((SPAN, 3 * rhs, every), F32),
@@ -504,9 +559,9 @@
         + [dma((max(ny - 1, 1),))] * 2
         + [dma((max(nz - 1, 1),))] * 2,
         compiler_params=pltpu.CompilerParams(
-            collective_id=0, has_side_effects=True, vmem_limit_bytes=32 * MIB
+            collective_id=0, has_side_effects=True, vmem_limit_bytes=44 * MIB
         ),
-    )(r, *matrices)
+    )(r, dense, pivots)
 
 
 def solve_kernel(k_in, rt, v, w, r, x_out, r_out):
@@ -549,8 +604,8 @@
     nr, nz = mesh.shape["rows"], mesh.shape["rhs"]
 
     def shards(right_side, tiles, pivots, columns):
-        matrices = setup(columns, tiles, pivots)
-        v, w, k, rt = krylov(nr, nz, right_side, matrices)
+        dense = assemble(columns, tiles)
+        v, w, k, rt = krylov(nr, nz, right_side, dense, pivots)
         return tuple(solve(k, rt, v, w, right_side))
 
     return jax.shard_map(

time: 99 us -> 96 us (0.970)
  Pallas kernels: 95 us -> 93 us
    pallas_call x1, Pallas kernels: 6.61 us -> 4.86 us  [assemble(): pl.pallas_call(assemble_kernel, out_shape=jax.ShapeDtypeStruct((3 * cells...]
where the time goes in v3:
time: 96 us; the launch traced here: 95.9 us
  Pallas kernels  93 us (97%)
  local copies, waits for them, and re-layouts  2.19 us (2%)
    pallas_call x1, Pallas kernels, krylov(): pl.pallas_call(functools.partial(krylov_kernel, nr, nz), out_shape=[jax.S...  75.7 us
    pallas_call x1, Pallas kernels, solve(): pl.pallas_call(solve_kernel, out_shape=[jax.ShapeDtypeStruct(r.shape, F32...  12.4 us
    pallas_call x1, Pallas kernels, assemble(): pl.pallas_call(assemble_kernel, out_shape=jax.ShapeDtypeStruct((3 * cells...  4.86 us
    unnamed x8, local copies, waits for them, and re-layouts  2.19 us

profile of v3, /device:TPU:4, one launch (start us, length us, event | category | flops | bytes accessed | tf_op | source)
XLA Modules:
  0.0 95.9 jit_solution(9633267308586077368)
XLA Ops:
  0.6 0.0 copy-start
  0.6 1.5 %copy-done = f32[8,7,64,64]{3,2,1,0:T(8,128)S(1)} copy-done((f32[8,7,64,64]{3,2,1,0:T(8,128)S(1)}, f32[8,7,64,64]{3,2,1,0:T(8,128)}, u32[]{:S(2)}) %copy-start) | copy-done | bytes 917528
  2.1 0.0 copy-start.3
  2.1 0.7 copy-done.3
  2.8 0.0 copy-start.1
  2.8 0.0 copy-start.2
  2.8 4.9 %shard_map.59.dense = f32[1536,512]{1,0:T(8,128)S(1)} custom-call(s32[8,7]{1,0:T(8,128)S(1)} %copy-done.3, f32[8,7,64,64]{3,2,1,0:T(8,128)S(1)} %copy-done), custom_call_target="tpu_custom_call" | custom-call | tf_op jit(solution)/shard_map/pallas_call | solution.py:69
  7.7 0.0 copy-done.1
  7.7 0.0 copy-done.2
  7.7 75.7 %shard_map.60 = (f32[128,512]{1,0:T(8,128)S(1)}, f32[128,512]{1,0:T(8,128)S(1)}, f32[128,128]{1,0:T(8,128)S(1)}, f32[8,128]{1,0:T(8,128)S(1)}) custom-call(f32[8,512]{1,0:T(8,128)S(1)} %copy-done.2, f32[1536,512]{1,0:T(8,128)S(1)} %shard_map.59.dense, f32[8,64,64]{2,1,0:T(8,128)S(1)} %copy-done.1), custom_call_target="tpu_custom_call" | custom-call | tf_op jit(solution)/shard_map/pallas_call | solution.py:533
  83.5 12.4 %shard_map.61 = (f32[8,512]{1,0:T(8,128)}, f32[8,512]{1,0:T(8,128)}) custom-call(f32[128,128]{1,0:T(8,128)S(1)} %get-tuple-element.6.k_in, f32[8,128]{1,0:T(8,128)S(1)} %get-tuple-element.7.rt, f32[128,512]{1,0:T(8,128)S(1)} %get-tuple-element.8.v, f32[128,512]{1,0:T(8,128)S(1)} %get-tuple-element.9.w, f32[8,512]{1,0:T(8,128)S(1)} %copy-done.2), custom_call_target="tpu_custom_call" | custom-call | tf_op jit(solution)/shard_map/pallas_call | solution.py:594
Async XLA Ops:
  0.6 1.5 %copy-start = (f32[8,7,64,64]{3,2,1,0:T(8,128)S(1)}, f32[8,7,64,64]{3,2,1,0:T(8,128)}, u32[]{:S(2)}) copy-start(f32[8,7,64,64]{3,2,1,0:T(8,128)} %tiles.1) | copy-start | bytes 2752516
  2.1 0.7 copy-start.3
  2.8 4.9 %copy-start.1 = (f32[8,64,64]{2,1,0:T(8,128)S(1)}, f32[8,64,64]{2,1,0:T(8,128)}, u32[]{:S(2)}) copy-start(f32[8,64,64]{2,1,0:T(8,128)} %pivots.1) | copy-start | bytes 393220
  2.8 4.9 %copy-start.2 = (f32[8,512]{1,0:T(8,128)S(1)}, f32[8,512]{1,0:T(8,128)}, u32[]{:S(2)}) copy-start(f32[8,512]{1,0:T(8,128)} %r.3) | copy-start | bytes 49156

commit v4 on v3

--- a/solution.py
+++ b/solution.py
@@ -48,34 +48,6 @@
     return total
 
 
-def assemble_kernel(cols, tiles, dense, held, sems):
-    rows, slots, bs = held.shape[0], held.shape[1], held.shape[2]
-    start = lax.axis_index("rows") * rows
-    copies = [pltpu.make_async_copy(tiles.at[i], held.at[i], sems.at[i]) for i in range(rows)]
-    for c in copies:
-        c.start()
-    dense[...] = jnp.zeros(dense.shape, F32)
-    for i in range(rows):
-        copies[i].wait()
-        for k in range(slots):
-            j = cols[i, k] - start + rows
-            at = (pl.ds(pl.multiple_of(j * bs, bs), bs), slice(i * bs, (i + 1) * bs))
-            dense[at] = dense[at] + held[i, k].T
-
-
-def assemble(cols, tiles):
-    rows, _, bs, _ = tiles.shape
-    cells = rows * bs
-    return pl.pallas_call(
-        assemble_kernel,
-        out_shape=jax.ShapeDtypeStruct((3 * cells, cells), F32),
-        in_specs=[SMEM, pl.BlockSpec(memory_space=pltpu.HBM)],
-        out_specs=VMEM,
-        scratch_shapes=[pltpu.VMEM(tiles.shape, F32), pltpu.SemaphoreType.DMA((rows,))],
-        compiler_params=pltpu.CompilerParams(vmem_limit_bytes=16 * MIB),
-    )(cols, tiles)
-
-
 def mul_parts(a, b):
     (ah, al), (bh, bl) = a, b
     return dot(ah, bh) + (dot(ah, bl) + dot(al, bh))
@@ -83,13 +55,13 @@
 
 def krylov_kernel(
     nr, nz,
-    r, dense, pivots,
+    cols, tiles, r, pivots,
     v_out, w_out, k_out, r_out,
-    dh, dm, dl, nh, nl, th, tl, sh, sl, tf, sf, pf,
+    held, dense, dh, dm, dl, nh, nl, th, tl, sh, sl, tf, sf, pf,
     va, wa, c, sv, other, joint,
     u_src, u_dst, s_src, s_dst, k_src, k_dst, w_src, w_dst, far, above, below,
     red_x, red_y, red_z,
-    link_send, link_recv, pair_send, pair_recv,
+    tile_sem, link_send, link_recv, pair_send, pair_recv,
     z_send, z_recv, x_send, x_recv, y_send, y_recv, k_send, k_recv,
 ):
     me, mz = lax.axis_index("rows"), lax.axis_index("rhs")
@@ -110,6 +82,10 @@
     def z_peer(o):
         return (me, lax.rem(mz + o, nz))
 
+    group, slots, bs = held.shape[0], held.shape[1], held.shape[2]
+    fetch = [pltpu.make_async_copy(tiles.at[i], held.at[i], tile_sem.at[i]) for i in range(group)]
+    for f in fetch:
+        f.start()
     barrier = pltpu.get_barrier_semaphore()
 
     def hello(device):
@@ -132,8 +108,30 @@
     def _():
         hello((me + 1, mz))
 
-    bs = pivots.shape[1]
     half = cells // 2
+
+    def block(i, j):
+        return (slice(i * bs, (i + 1) * bs), slice(j * bs, (j + 1) * bs))
+
+    nothing = jnp.zeros((bs, bs), F32)
+    for i in range(group):
+        fetch[i].wait()
+        away = [cols[i, k] - cols[i, 0] for k in range(1, slots)]
+        for delta in range(-group, group + 1):
+            tile = held[i, 0] if delta == 0 else None
+            for k in range(1, slots):
+                term = held[i, k] * (away[k - 1] == delta).astype(F32)
+                tile = term if tile is None else tile + term
+            j = i + delta
+            if 0 <= j < group:
+                dense[block(group + i, j)] = tile
+            else:
+                dense[block(group + j, i)] = tile.T
+        for j in range(group):
+            if j < i:
+                dense[block(j, i)] = nothing
+            if j > i:
+                dense[block(2 * group + j, i)] = nothing
 
     def block_diagonal(first_row):
         zero = jnp.zeros((bs, bs), F32)
@@ -216,6 +214,10 @@
             s.start()
         begun.extend(copies)
 
+    def values(refs, rows=slice(None)):
+        return [ref[rows] for ref in refs]
+
+    n_refs, t_refs, s_refs = (nh, nl), (th, tl), (sh, sl)
     turn = chip == chips - 1
     ahead = chip < chips - 1
     pair_n = copy(tf, other, pair_send.at[0], pair_recv.at[0], (me - 1, mz))
@@ -224,6 +226,20 @@
     @pl.when(odd & ahead)
     def _():
         pair_n.start()
+
+    at_once = links(0)
+
+    @pl.when(first)
+    def _():
+        w_src[0] = times(r[...], values(t_refs))
+        at_once["w"].start()
+
+    @pl.when(pos == 1)
+    def _():
+        at_once["w"].wait_recv()
+        c[...] = r[...] - w_dst[0]
+        u_src[0] = times(c[...], values(t_refs))
+        at_once["u"].start()
 
     low = mul(fb.T, pf[half:cells])
     sf[half:cells] = low
@@ -246,10 +262,6 @@
     def _():
         above[...] = jnp.zeros(above.shape, F32)
 
-    def values(refs, rows=slice(None)):
-        return [ref[rows] for ref in refs]
-
-    n_refs, t_refs, s_refs = (nh, nl), (th, tl), (sh, sl)
     kt_refs, k_refs = (joint.at[0], joint.at[1]), (joint.at[2], joint.at[3])
 
     def split_dense():
@@ -299,15 +311,10 @@
             def _():
                 split_dense()
 
-        @pl.when(odd)
+        @pl.when(odd & (chip >= begins))
         def _():
             at["w"].wait_recv()
             c[...] = source[...] - w_dst[m]
-
-        @pl.when(odd & (chip < begins))
-        def _():
-            u_src[m] = times(c[...], values(t_refs))
-            at["u"].start()
 
         @pl.when(odd & ahead)
         def _():
@@ -356,7 +363,7 @@
             k_src[m] = times(c[...], values(kt_refs))
             at["k"].start()
 
-        @pl.when(even & ahead)
+        @pl.when(even & ahead & (chip >= begins))
         def _():
             w_src[m] = times(c[...], values(t_refs))
             at["w"].start()
@@ -522,7 +529,7 @@
                 at[name].wait_send()
 
 
-def krylov(nr, nz, r, dense, pivots):
+def krylov(nr, nz, cols, tiles, r, pivots):
     rhs, cells = r.shape
     ny = nr // SPAN
     dma = pltpu.SemaphoreType.DMA
@@ -538,9 +545,10 @@
             jax.ShapeDtypeStruct((every, every), F32),
             jax.ShapeDtypeStruct((rhs, every), F32),
         ],
-        in_specs=[VMEM] * 3,
+        in_specs=[SMEM, pl.BlockSpec(memory_space=pltpu.HBM), VMEM, VMEM],
         out_specs=[VMEM] * 4,
-        scratch_shapes=[pltpu.VMEM((3 * cells, cells), BF)] * 3
+        scratch_shapes=[pltpu.VMEM(tiles.shape, F32), pltpu.VMEM((3 * cells, cells), F32)]
+        + [pltpu.VMEM((3 * cells, cells), BF)] * 3
         + [square_half] * 6
         + [square] * 3
         + [pltpu.VMEM((nz, 2, rhs, cells), F32)] * 2
@@ -552,6 +560,7 @@
             pltpu.VMEM((ny, 3 * rhs, every), F32),
             pltpu.VMEM((nz, 2 * rhs, every), F32),
         ]
+        + [dma((tiles.shape[0],))]
         + [dma((7, 2))] * 2
         + [dma((2,))] * 2
         + [dma((4, max(nz - 1, 1)))] * 2
@@ -561,7 +570,37 @@
         compiler_params=pltpu.CompilerParams(
             collective_id=0, has_side_effects=True, vmem_limit_bytes=44 * MIB
         ),
-    )(r, dense, pivots)
+    )(cols, tiles, r, pivots)
+
+
+def spd_inverse(k, block):
+    size = k.shape[0]
+    row_of = lax.broadcasted_iota(jnp.int32, (size, 1), 0)
+    col_of = lax.broadcasted_iota(jnp.int32, (1, size), 1)
+    span = range(block)
+    for b in range(0, size, block):
+        d = [[jnp.broadcast_to(k[b + i : b + i + 1, b + j : b + j + 1], (1, size)) for j in span] for i in span]
+        for p in span:
+            inv = 1.0 / d[p][p]
+            row = [inv if j == p else d[p][j] * inv for j in span]
+            for i in span:
+                if i != p:
+                    f = d[i][p]
+                    d[i] = [-f * row[p] if j == p else d[i][j] - f * row[j] for j in span]
+            d[p] = row
+        in_cols = (col_of >= b) & (col_of < b + block)
+        in_rows = (row_of >= b) & (row_of < b + block)
+        base = jnp.where(in_rows | in_cols, 0.0, k)
+        for i in span:
+            row, corner = d[i][0] * k[b : b + 1, :], d[i][0]
+            for j in range(1, block):
+                row = row + d[i][j] * k[b + j : b + j + 1, :]
+                corner = jnp.where(col_of == b + j, d[i][j], corner)
+            row = jnp.where(in_cols, corner, row)
+            col = jnp.where(in_rows, jnp.where(row_of == b + i, -1.0, 0.0), k[:, b + i : b + i + 1])
+            base = base - col * row
+        k = base
+    return k
 
 
 def solve_kernel(k_in, rt, v, w, r, x_out, r_out):
@@ -573,19 +612,8 @@
     row_p, col_p = lax.rem(row_of // 8, 2) == 1, lax.rem(col_of // 8, 2) == 1
     both = k + kt
     k = jnp.where(row_p, jnp.where(col_p, both, kt), jnp.where(col_p, k, 0.5 * both))
-    for i in range(0, size, 2):
-        j = i + 1
-        a, b, d = k[i : i + 1, i : i + 1], k[i : i + 1, j : j + 1], k[j : j + 1, j : j + 1]
-        inv = 1.0 / (a * d - b * b)
-        ra = jnp.where(col_of == i, 1.0, jnp.where(col_of == j, 0.0, k[i : i + 1, :]))
-        rb = jnp.where(col_of == j, 1.0, jnp.where(col_of == i, 0.0, k[j : j + 1, :]))
-        new_a, new_b = (d * ra - b * rb) * inv, (a * rb - b * ra) * inv
-        ca = jnp.where(row_of == i, -1.0, jnp.where(row_of == j, 0.0, k[:, i : i + 1]))
-        cb = jnp.where(row_of == j, -1.0, jnp.where(row_of == i, 0.0, k[:, j : j + 1]))
-        gone = (row_of == i) | (row_of == j) | (col_of == i) | (col_of == j)
-        k = jnp.where(gone, 0.0, k) - ca * new_a - cb * new_b
     high = lax.Precision.HIGHEST
-    c = jnp.dot(rt[...], k, precision=high, preferred_element_type=F32)
+    c = jnp.dot(rt[...], spd_inverse(k, 4), precision=high, preferred_element_type=F32)
     x_out[...] = jnp.dot(c, v[...], precision=high, preferred_element_type=F32)
     r_out[...] = r[...] - jnp.dot(c, w[...], precision=high, preferred_element_type=F32)
 
@@ -604,8 +632,7 @@
     nr, nz = mesh.shape["rows"], mesh.shape["rhs"]
 
     def shards(right_side, tiles, pivots, columns):
-        dense = assemble(columns, tiles)
-        v, w, k, rt = krylov(nr, nz, right_side, dense, pivots)
+        v, w, k, rt = krylov(nr, nz, columns, tiles, right_side, pivots)
         return tuple(solve(k, rt, v, w, right_side))
 
     return jax.shard_map(

time: 96 us -> 88.8 us (0.925)
  Pallas kernels: 93 us -> 84.1 us
  local copies, waits for them, and re-layouts: 2.19 us -> 3.85 us
    pallas_call x1, Pallas kernels: 12.4 us -> 5.7 us  [solve(): pl.pallas_call(solve_kernel, out_shape=[jax.ShapeDtypeStruct(r.shape, F32...]
    pallas_call x1 -> x0, Pallas kernels: 4.86 us -> none  [assemble(): pl.pallas_call(assemble_kernel, out_shape=jax.ShapeDtypeStruct((3 * cells...]
    pallas_call x1, Pallas kernels: 75.7 us -> 78.4 us  [krylov(): pl.pallas_call(functools.partial(krylov_kernel, nr, nz), out_shape=[jax.S...]
    unnamed x8, local copies, waits for them, and re-layouts: 2.19 us -> 3.85 us
where the time goes in v4:
time: 88.8 us; the launch traced here: 88.6 us
  Pallas kernels  84.1 us (95%)
  local copies, waits for them, and re-layouts  3.85 us (4%)
    pallas_call x1, Pallas kernels, krylov(): pl.pallas_call(functools.partial(krylov_kernel, nr, nz), out_shape=[jax.S...  78.4 us
    pallas_call x1, Pallas kernels, solve(): pl.pallas_call(solve_kernel, out_shape=[jax.ShapeDtypeStruct(r.shape, F32...  5.7 us
    unnamed x8, local copies, waits for them, and re-layouts  3.85 us

profile of v4, /device:TPU:4, one launch (start us, length us, event | category | flops | bytes accessed | tf_op | source)
XLA Modules:
  0.0 88.6 jit_solution(5141266822016920393)
XLA Ops:
  0.6 0.0 copy-start
  0.6 1.5 %copy-done = f32[8,7,64,64]{3,2,1,0:T(8,128)S(1)} copy-done((f32[8,7,64,64]{3,2,1,0:T(8,128)S(1)}, f32[8,7,64,64]{3,2,1,0:T(8,128)}, u32[]{:S(2)}) %copy-start) | copy-done | bytes 917528
  2.1 0.0 copy-start.1
  2.1 0.9 %copy-done.1 = f32[8,64,64]{2,1,0:T(8,128)S(1)} copy-done((f32[8,64,64]{2,1,0:T(8,128)S(1)}, f32[8,64,64]{2,1,0:T(8,128)}, u32[]{:S(2)}) %copy-start.1) | copy-done | bytes 131096
  3.1 0.0 copy-start.2
  3.1 0.7 copy-done.2
  3.8 0.0 copy-start.3
  3.8 0.7 copy-done.3
  4.5 78.4 %shard_map.59 = (f32[128,512]{1,0:T(8,128)S(1)}, f32[128,512]{1,0:T(8,128)S(1)}, f32[128,128]{1,0:T(8,128)S(1)}, f32[8,128]{1,0:T(8,128)S(1)}) custom-call(s32[8,7]{1,0:T(8,128)S(1)} %copy-done.3, f32[8,7,64,64]{3,2,1,0:T(8,128)S(1)} %copy-done, f32[8,512]{1,0:T(8,128)S(1)} %copy-done.2, f32[8,64,64]{2,1,0:T(8,128)S(1)} %copy-done.1), custom_call_target="tpu_custom_call" | custom-call | tf_op jit(solution)/shard_map/pallas_call | solution.py:540
  82.9 5.7 %shard_map.60 = (f32[8,512]{1,0:T(8,128)}, f32[8,512]{1,0:T(8,128)}) custom-call(f32[128,128]{1,0:T(8,128)S(1)} %get-tuple-element.6.k_in, f32[8,128]{1,0:T(8,128)S(1)} %get-tuple-element.7.rt, f32[128,512]{1,0:T(8,128)S(1)} %get-tuple-element.8.v, f32[128,512]{1,0:T(8,128)S(1)} %get-tuple-element.9.w, f32[8,512]{1,0:T(8,128)S(1)} %copy-done.2), custom_call_target="tpu_custom_call" | custom-call | tf_op jit(solution)/shard_map/pallas_call | solution.py:622
Async XLA Ops:
  0.6 1.5 %copy-start = (f32[8,7,64,64]{3,2,1,0:T(8,128)S(1)}, f32[8,7,64,64]{3,2,1,0:T(8,128)}, u32[]{:S(2)}) copy-start(f32[8,7,64,64]{3,2,1,0:T(8,128)} %tiles.1) | copy-start | bytes 2752516
  2.1 0.9 %copy-start.1 = (f32[8,64,64]{2,1,0:T(8,128)S(1)}, f32[8,64,64]{2,1,0:T(8,128)}, u32[]{:S(2)}) copy-start(f32[8,64,64]{2,1,0:T(8,128)} %pivots.1) | copy-start | bytes 393220
  3.1 0.7 copy-start.2
  3.8 0.7 copy-start.3

commit v5 on v4

--- a/solution.py
+++ b/solution.py
@@ -55,13 +55,13 @@
 
 def krylov_kernel(
     nr, nz,
-    cols, tiles, r, pivots,
+    cols_in, tiles, r_in, pivots_in,
     v_out, w_out, k_out, r_out,
-    held, dense, dh, dm, dl, nh, nl, th, tl, sh, sl, tf, sf, pf,
+    cols, r, pivots, held, dense, dh, dm, dl, nh, nl, th, tl, sh, sl, tf, sf, pf,
     va, wa, c, sv, other, joint,
     u_src, u_dst, s_src, s_dst, k_src, k_dst, w_src, w_dst, far, above, below,
     red_x, red_y, red_z,
-    tile_sem, link_send, link_recv, pair_send, pair_recv,
+    tile_sem, in_sem, link_send, link_recv, pair_send, pair_recv,
     z_send, z_recv, x_send, x_recv, y_send, y_recv, k_send, k_recv,
 ):
     me, mz = lax.axis_index("rows"), lax.axis_index("rhs")
@@ -84,7 +84,9 @@
 
     group, slots, bs = held.shape[0], held.shape[1], held.shape[2]
     fetch = [pltpu.make_async_copy(tiles.at[i], held.at[i], tile_sem.at[i]) for i in range(group)]
-    for f in fetch:
+    whole = ((cols_in, cols), (pivots_in, pivots), (r_in, r))
+    fetch += [pltpu.make_async_copy(src, dst, in_sem.at[i]) for i, (src, dst) in enumerate(whole)]
+    for f in fetch[group:] + fetch[:group]:
         f.start()
     barrier = pltpu.get_barrier_semaphore()
 
@@ -114,6 +116,8 @@
         return (slice(i * bs, (i + 1) * bs), slice(j * bs, (j + 1) * bs))
 
     nothing = jnp.zeros((bs, bs), F32)
+    for f in fetch[group:]:
+        f.wait()
     for i in range(group):
         fetch[i].wait()
         away = [cols[i, k] - cols[i, 0] for k in range(1, slots)]
@@ -488,9 +492,9 @@
     begin(over_y)
     for s in over_y:
         s.wait_recv()
-    whole = total(red_y, ny)
-    r_out[...] = whole[16:24]
-    red_z[mz] = whole[0:16]
+    both = total(red_y, ny)
+    r_out[...] = both[16:24]
+    red_z[mz] = both[0:16]
     over_z = spread(red_z, mz, k_send, k_recv, z_peer, nz)
     begin(over_z)
     for m in range(2):
@@ -545,9 +549,10 @@
             jax.ShapeDtypeStruct((every, every), F32),
             jax.ShapeDtypeStruct((rhs, every), F32),
         ],
-        in_specs=[SMEM, pl.BlockSpec(memory_space=pltpu.HBM), VMEM, VMEM],
+        in_specs=[pl.BlockSpec(memory_space=pltpu.HBM)] * 4,
         out_specs=[VMEM] * 4,
-        scratch_shapes=[pltpu.VMEM(tiles.shape, F32), pltpu.VMEM((3 * cells, cells), F32)]
+        scratch_shapes=[pltpu.SMEM(cols.shape, jnp.int32), vector, pltpu.VMEM(pivots.shape, F32)]
+        + [pltpu.VMEM(tiles.shape, F32), pltpu.VMEM((3 * cells, cells), F32)]
         + [pltpu.VMEM((3 * cells, cells), BF)] * 3
         + [square_half] * 6
         + [square] * 3
@@ -560,7 +565,7 @@
             pltpu.VMEM((ny, 3 * rhs, every), F32),
             pltpu.VMEM((nz, 2 * rhs, every), F32),
         ]
-        + [dma((tiles.shape[0],))]
+        + [dma((tiles.shape[0],)), dma((3,))]
         + [dma((7, 2))] * 2
         + [dma((2,))] * 2
         + [dma((4, max(nz - 1, 1)))] * 2
@@ -568,7 +573,7 @@
         + [dma((max(ny - 1, 1),))] * 2
         + [dma((max(nz - 1, 1),))] * 2,
         compiler_params=pltpu.CompilerParams(
-            collective_id=0, has_side_effects=True, vmem_limit_bytes=44 * MIB
+            collective_id=0, has_side_effects=True, vmem_limit_bytes=60 * MIB
         ),
     )(cols, tiles, r, pivots)
 
@@ -603,9 +608,14 @@
     return k
 
 
-def solve_kernel(k_in, rt, v, w, r, x_out, r_out):
-    size = k_in.shape[0]
-    k = k_in[...]
+def solve_kernel(k_in, rt_in, v_in, w_in, r_in, x_out, r_out, k_buf, rt, v, w, r, sems):
+    whole = ((k_in, k_buf), (rt_in, rt), (v_in, v), (w_in, w), (r_in, r))
+    fetch = [pltpu.make_async_copy(src, dst, sems.at[i]) for i, (src, dst) in enumerate(whole)]
+    for f in fetch:
+        f.start()
+    fetch[0].wait()
+    size = k_buf.shape[0]
+    k = k_buf[...]
     kt = k.T
     row_of = lax.broadcasted_iota(jnp.int32, (size, 1), 0)
     col_of = lax.broadcasted_iota(jnp.int32, (1, size), 1)
@@ -613,19 +623,24 @@
     both = k + kt
     k = jnp.where(row_p, jnp.where(col_p, both, kt), jnp.where(col_p, k, 0.5 * both))
     high = lax.Precision.HIGHEST
-    c = jnp.dot(rt[...], spd_inverse(k, 4), precision=high, preferred_element_type=F32)
+    inverse = spd_inverse(k, 4)
+    for f in fetch[1:]:
+        f.wait()
+    c = jnp.dot(rt[...], inverse, precision=high, preferred_element_type=F32)
     x_out[...] = jnp.dot(c, v[...], precision=high, preferred_element_type=F32)
     r_out[...] = r[...] - jnp.dot(c, w[...], precision=high, preferred_element_type=F32)
 
 
 def solve(k, rt, v, w, r):
+    operands = (k, rt, v, w, r)
     return pl.pallas_call(
         solve_kernel,
         out_shape=[jax.ShapeDtypeStruct(r.shape, F32)] * 2,
-        in_specs=[VMEM] * 5,
+        in_specs=[pl.BlockSpec(memory_space=pltpu.HBM)] * 5,
         out_specs=[VMEM] * 2,
-        compiler_params=pltpu.CompilerParams(vmem_limit_bytes=16 * MIB),
-    )(k, rt, v, w, r)
+        scratch_shapes=[pltpu.VMEM(o.shape, F32) for o in operands] + [pltpu.SemaphoreType.DMA((5,))],
+        compiler_params=pltpu.CompilerParams(vmem_limit_bytes=60 * MIB),
+    )(*operands)
 
 
 def solution(mesh):

time: 88.8 us -> 85 us (0.957)
  local copies, waits for them, and re-layouts: 3.85 us -> 0 us
    unnamed x8 -> x0, local copies, waits for them, and re-layouts: 3.85 us -> none
where the time goes in v5:
time: 85 us; the launch traced here: 84.8 us
  Pallas kernels  84 us (99%)
    pallas_call x1, Pallas kernels, krylov(): pl.pallas_call(functools.partial(krylov_kernel, nr, nz), out_shape=[jax.S...  77.5 us
    pallas_call x1, Pallas kernels, solve(): pl.pallas_call(solve_kernel, out_shape=[jax.ShapeDtypeStruct(r.shape, F32...  6.48 us

profile of v5, /device:TPU:4, one launch (start us, length us, event | category | flops | bytes accessed | tf_op | source)
XLA Modules:
  0.0 84.8 jit_solution(15915088221505674816)
XLA Ops:
  0.6 77.5 %shard_map.59 = (f32[128,512]{1,0:T(8,128)}, f32[128,512]{1,0:T(8,128)}, f32[128,128]{1,0:T(8,128)}, f32[8,128]{1,0:T(8,128)}) custom-call(s32[8,7]{1,0:T(8,128)} %cols_in.1, f32[8,7,64,64]{3,2,1,0:T(8,128)} %tiles.1, f32[8,512]{1,0:T(8,128)} %r_in.3, f32[8,64,64]{2,1,0:T(8,128)} %pivots_in.1), custom_call_target="tpu_custom_call" | custom-call | tf_op jit(solution)/shard_map/pallas_call | solution.py:544
  78.1 6.5 %shard_map.60 = (f32[8,512]{1,0:T(8,128)}, f32[8,512]{1,0:T(8,128)}) custom-call(f32[128,128]{1,0:T(8,128)} %get-tuple-element.6.k_in, f32[8,128]{1,0:T(8,128)} %get-tuple-element.7.rt_in, f32[128,512]{1,0:T(8,128)} %get-tuple-element.8.v_in, f32[128,512]{1,0:T(8,128)} %get-tuple-element.9.w_in, f32[8,512]{1,0:T(8,128)} %r_in.3), custom_call_target="tpu_custom_call" | custom-call | tf_op jit(solution)/shard_map/pallas_call | solution.py:636

commit v6 on v5

--- a/solution.py
+++ b/solution.py
@@ -58,8 +58,9 @@
     cols_in, tiles, r_in, pivots_in,
     v_out, w_out, k_out, r_out,
     cols, r, pivots, held, dense, dh, dm, dl, nh, nl, th, tl, sh, sl, tf, sf, pf,
-    va, wa, c, sv, other, joint,
+    va, wa, c, sv, other, third, joint,
     u_src, u_dst, s_src, s_dst, k_src, k_dst, w_src, w_dst, far, above, below,
+    g_src, g_dst, h_dst, e_src, e_dst,
     red_x, red_y, red_z,
     tile_sem, in_sem, link_send, link_recv, pair_send, pair_recv,
     z_send, z_recv, x_send, x_recv, y_send, y_recv, k_send, k_recv,
@@ -198,6 +199,9 @@
             far=link(4, m, z, far, me - 2),
             back=link(5, m, z, above, me - 1),
             on=link(6, m, z, below, me + 1),
+            g=link(7, m, g_src.at[m], g_dst, me + 4),
+            h=link(8, m, z, h_dst, me - 4),
+            e=link(9, m, e_src.at[m], e_dst, me - 2),
         )
 
     def to_z(array, m, kind):
@@ -231,6 +235,7 @@
     def _():
         pair_n.start()
 
+    pair_k = copy(other, third, pair_send.at[2], pair_recv.at[2], (me - 2, mz))
     at_once = links(0)
 
     @pl.when(first)
@@ -245,14 +250,34 @@
         u_src[0] = times(c[...], values(t_refs))
         at_once["u"].start()
 
-    low = mul(fb.T, pf[half:cells])
-    sf[half:cells] = low
-    sh[half:cells], sl[half:cells] = parts(low, 2)
-    high = mul(fx.T, pf[half:cells])
-    corner = mul(fa.T, pf[0:half, 0:half])
-    high = jnp.concatenate([high[:, 0:half] + corner, high[:, half:cells]], axis=1)
-    sf[0:half] = high
-    sh[0:half], sl[0:half] = parts(high, 2)
+    def middle():
+        low = mul(fb.T, pf[half:cells])
+        sf[half:cells] = low
+        sh[half:cells], sl[half:cells] = parts(low, 2)
+        high = mul(fx.T, pf[half:cells])
+        corner = mul(fa.T, pf[0:half, 0:half])
+        high = jnp.concatenate([high[:, 0:half] + corner, high[:, half:cells]], axis=1)
+        sf[0:half] = high
+        sh[0:half], sl[0:half] = parts(high, 2)
+
+    kt_refs, k_refs = (joint.at[0], joint.at[1]), (joint.at[2], joint.at[3])
+    two_t, two = (joint.at[4], joint.at[5]), (joint.at[6], joint.at[7])
+
+    @pl.when(even & ahead)
+    def _():
+        pair_n.wait_recv()
+        kt = mul_parts(values(t_refs), parts(other[...], 2))
+        for ref, p in zip(kt_refs, parts(kt, 2)):
+            ref[...] = p
+        other[...] = kt
+
+    @pl.when(pos == 4)
+    def _():
+        pair_k.start()
+
+    @pl.when(pos != 2)
+    def _():
+        middle()
 
     @pl.when(last)
     def _():
@@ -266,7 +291,6 @@
     def _():
         above[...] = jnp.zeros(above.shape, F32)
 
-    kt_refs, k_refs = (joint.at[0], joint.at[1]), (joint.at[2], joint.at[3])
 
     def split_dense():
         for i in range(3):
@@ -274,14 +298,6 @@
             for ref, p in zip((dh, dm, dl), parts(dense[rows], 3)):
                 ref[rows] = p
 
-    @pl.when(even & ahead)
-    def _():
-        pair_n.wait_recv()
-        kt = mul_parts(values(t_refs), parts(other[...], 2))
-        for ref, p in zip(kt_refs, parts(kt, 2)):
-            ref[...] = p
-        other[...] = kt
-
     @pl.when(even & turn)
     def _():
         pair_s.wait_recv()
@@ -311,7 +327,7 @@
 
         if m == 0:
 
-            @pl.when(jnp.logical_not(first) & (pos != 1))
+            @pl.when((pos > 2))
             def _():
                 split_dense()
 
@@ -357,12 +373,32 @@
             at["u"].wait_recv()
             c[...] = source[...] - u_dst[m]
 
+        direct = m == 1
+        if direct:
+
+            @pl.when(pos == 4)
+            def _():
+                k_src[m] = times(c[...], values(kt_refs))
+                at["k"].start()
+
         @pl.when(even & (chip > begins))
         def _():
             at["k"].wait_recv()
             c[...] = c[...] + k_dst[m]
 
-        @pl.when(even & ahead & (chip >= begins))
+        if direct:
+
+            @pl.when(pos == 6)
+            def _():
+                at["g"].wait_recv()
+                c[...] = c[...] + g_dst[m]
+
+            @pl.when(pos == 2)
+            def _():
+                g_src[m] = times(c[...], values(two_t))
+                at["g"].start()
+
+        @pl.when(even & ahead & (chip >= begins) & ((pos != 4) if direct else (pos >= 0)))
         def _():
             k_src[m] = times(c[...], values(kt_refs))
             at["k"].start()
@@ -374,11 +410,15 @@
 
         if m == 0:
 
+            @pl.when(pos == 2)
+            def _():
+                middle()
+
             @pl.when(even & ahead)
             def _():
                 back_product()
 
-            @pl.when(first)
+            @pl.when(even & (pos <= 2))
             def _():
                 split_dense()
 
@@ -386,6 +426,23 @@
         def _():
             other_half()
             c[...] = times(c[...], values(s_refs)) - sv[...]
+
+        if direct:
+
+            @pl.when(pos == 4)
+            def _():
+                e_src[m] = c[...]
+                at["e"].start()
+
+            @pl.when(pos == 2)
+            def _():
+                at["e"].wait_recv()
+                c[...] = c[...] + times(e_dst[m], values(k_refs))
+                at["h"].wait_recv()
+                va[mz, m] = c[...] + times(h_dst[m], values(two))
+
+        @pl.when(even & ahead & ((pos != 2) if direct else (pos >= 0)))
+        def _():
             at["far"].wait_recv()
             va[mz, m] = c[...] + times(far[m], values(k_refs))
 
@@ -393,7 +450,13 @@
         def _():
             va[mz, m] = times(c[...], values(s_refs)) - sv[...]
 
-        @pl.when(even & (chip > 0))
+        if direct:
+
+            @pl.when(pos == 6)
+            def _():
+                at["h"].start()
+
+        @pl.when(even & (chip > 0) & ((pos != 4) if direct else (pos >= 0)))
         def _():
             at["far"].start()
 
@@ -411,6 +474,17 @@
             at["on"].start()
 
         begin(to_z(va, m, 2 * m))
+
+        if m == 0:
+
+            @pl.when(pos == 2)
+            def _():
+                pair_k.wait_recv()
+                t = mul_parts(values(kt_refs), parts(third[...], 2))
+                for ref, p in zip(two_t, parts(t, 2)):
+                    ref[...] = p
+                for ref, p in zip(two, parts(t.T, 2)):
+                    ref[...] = p
 
         d = (dh, dm, dl)
 
@@ -516,6 +590,10 @@
     def _():
         pair_s.wait_send()
 
+    @pl.when(pos == 4)
+    def _():
+        pair_k.wait_send()
+
     for m in range(2):
         at = links(m)
         for name, started in (
@@ -523,7 +601,10 @@
             ("s", odd),
             ("k", even & ahead & (chip >= (1 if m == 0 else 0))),
             ("w", even),
-            ("far", even & (chip > 0)),
+            ("far", even & (chip > 0) & ((pos != 4) if m == 1 else (pos >= 0))),
+            ("g", (pos == 2) & (m == 1)),
+            ("h", (pos == 6) & (m == 1)),
+            ("e", (pos == 4) & (m == 1)),
             ("back", has_before),
             ("on", has_next),
         ):
@@ -558,16 +639,16 @@
         + [square] * 3
         + [pltpu.VMEM((nz, 2, rhs, cells), F32)] * 2
         + [vector] * 2
-        + [square, pltpu.VMEM((4, cells, cells), BF)]
-        + [vectors] * 11
+        + [square, square, pltpu.VMEM((8, cells, cells), BF)]
+        + [vectors] * 16
         + [
             pltpu.VMEM((SPAN, 3 * rhs, every), F32),
             pltpu.VMEM((ny, 3 * rhs, every), F32),
             pltpu.VMEM((nz, 2 * rhs, every), F32),
         ]
         + [dma((tiles.shape[0],)), dma((3,))]
-        + [dma((7, 2))] * 2
-        + [dma((2,))] * 2
+        + [dma((10, 2))] * 2
+        + [dma((3,))] * 2
         + [dma((4, max(nz - 1, 1)))] * 2
         + [dma((SPAN - 1,))] * 2
         + [dma((max(ny - 1, 1),))] * 2

time: 85 us -> 84.1 us (0.989)
  Pallas kernels: 84 us -> 83.1 us
    pallas_call x1, Pallas kernels: 77.5 us -> 76.6 us  [krylov(): pl.pallas_call(functools.partial(krylov_kernel, nr, nz), out_shape=[jax.S...]
where the time goes in v6:
time: 84.1 us; the launch traced here: 83.9 us
  Pallas kernels  83.1 us (99%)
    pallas_call x1, Pallas kernels, krylov(): pl.pallas_call(functools.partial(krylov_kernel, nr, nz), out_shape=[jax.S...  76.6 us
    pallas_call x1, Pallas kernels, solve(): pl.pallas_call(solve_kernel, out_shape=[jax.ShapeDtypeStruct(r.shape, F32...  6.48 us

profile of v6, /device:TPU:4, one launch (start us, length us, event | category | flops | bytes accessed | tf_op | source)
XLA Modules:
  0.0 83.9 jit_solution(8578879481550929994)
XLA Ops:
  0.6 76.6 %shard_map.59 = (f32[128,512]{1,0:T(8,128)}, f32[128,512]{1,0:T(8,128)}, f32[128,128]{1,0:T(8,128)}, f32[8,128]{1,0:T(8,128)}) custom-call(s32[8,7]{1,0:T(8,128)} %cols_in.1, f32[8,7,64,64]{3,2,1,0:T(8,128)} %tiles.1, f32[8,512]{1,0:T(8,128)} %r_in.3, f32[8,64,64]{2,1,0:T(8,128)} %pivots_in.1), custom_call_target="tpu_custom_call" | custom-call | tf_op jit(solution)/shard_map/pallas_call | solution.py:625
  77.3 6.5 %shard_map.60 = (f32[8,512]{1,0:T(8,128)}, f32[8,512]{1,0:T(8,128)}) custom-call(f32[128,128]{1,0:T(8,128)} %get-tuple-element.6.k_in, f32[8,128]{1,0:T(8,128)} %get-tuple-element.7.rt_in, f32[128,512]{1,0:T(8,128)} %get-tuple-element.8.v_in, f32[128,512]{1,0:T(8,128)} %get-tuple-element.9.w_in, f32[8,512]{1,0:T(8,128)} %r_in.3), custom_call_target="tpu_custom_call" | custom-call | tf_op jit(solution)/shard_map/pallas_call | solution.py:717

commit v7 on v6

--- a/solution.py
+++ b/solution.py
@@ -235,7 +235,10 @@
     def _():
         pair_n.start()
 
-    pair_k = copy(other, third, pair_send.at[2], pair_recv.at[2], (me - 2, mz))
+    pair_k = [
+        copy(other.at[part], third.at[part], pair_send.at[2 + i], pair_recv.at[2 + i], (me - 2, mz))
+        for i, part in enumerate((slice(0, half), slice(half, cells)))
+    ]
     at_once = links(0)
 
     @pl.when(first)
@@ -273,7 +276,7 @@
 
     @pl.when(pos == 4)
     def _():
-        pair_k.start()
+        pair_k[0].start()
 
     @pl.when(pos != 2)
     def _():
@@ -331,6 +334,15 @@
             def _():
                 split_dense()
 
+        early = to_z(va, 0, 0) + to_z(wa, 0, 1) if m == 1 else []
+
+        if m == 1:
+
+            @pl.when(odd | (chip >= chips - 2))
+            def _():
+                for s in early:
+                    s.start()
+
         @pl.when(odd & (chip >= begins))
         def _():
             at["w"].wait_recv()
@@ -408,6 +420,14 @@
             w_src[m] = times(c[...], values(t_refs))
             at["w"].start()
 
+        if m == 1:
+
+            @pl.when(even & (chip < chips - 2))
+            def _():
+                for s in early:
+                    s.start()
+
+        begun.extend(early)
         if m == 0:
 
             @pl.when(pos == 2)
@@ -473,18 +493,14 @@
         def _():
             at["on"].start()
 
-        begin(to_z(va, m, 2 * m))
+        if m == 1:
+            begin(to_z(va, 1, 2))
 
         if m == 0:
 
-            @pl.when(pos == 2)
-            def _():
-                pair_k.wait_recv()
-                t = mul_parts(values(kt_refs), parts(third[...], 2))
-                for ref, p in zip(two_t, parts(t, 2)):
-                    ref[...] = p
-                for ref, p in zip(two, parts(t.T, 2)):
-                    ref[...] = p
+            @pl.when(pos == 4)
+            def _():
+                pair_k[1].start()
 
         d = (dh, dm, dl)
 
@@ -551,7 +567,21 @@
             wa[mz, m] = part(below[m], 0)
 
         wa[mz, m] = c[...] + sv[...] + wa[mz, m]
-        begin(to_z(wa, m, 2 * m + 1))
+        if m == 1:
+            begin(to_z(wa, 1, 3))
+
+        else:
+
+            @pl.when(pos == 2)
+            def _():
+                for p in pair_k:
+                    p.wait_recv()
+                t = mul_parts(values(kt_refs), parts(third[...], 2))
+                for ref, p in zip(two_t, parts(t, 2)):
+                    ref[...] = p
+                for ref, p in zip(two, parts(t.T, 2)):
+                    ref[...] = p
+
 
     def total(array, count):
         value = array[0]
@@ -592,7 +622,8 @@
 
     @pl.when(pos == 4)
     def _():
-        pair_k.wait_send()
+        for p in pair_k:
+            p.wait_send()
 
     for m in range(2):
         at = links(m)
@@ -648,7 +679,7 @@
         ]
         + [dma((tiles.shape[0],)), dma((3,))]
         + [dma((10, 2))] * 2
-        + [dma((3,))] * 2
+        + [dma((4,))] * 2
         + [dma((4, max(nz - 1, 1)))] * 2
         + [dma((SPAN - 1,))] * 2
         + [dma((max(ny - 1, 1),))] * 2

time: 84.1 us -> 81.6 us (0.970)
  Pallas kernels: 83.1 us -> 80.7 us
    pallas_call x1, Pallas kernels: 76.6 us -> 74.2 us  [krylov(): pl.pallas_call(functools.partial(krylov_kernel, nr, nz), out_shape=[jax.S...]
where the time goes in v7:
time: 81.6 us; the launch traced here: 81.5 us
  Pallas kernels  80.7 us (99%)
    pallas_call x1, Pallas kernels, krylov(): pl.pallas_call(functools.partial(krylov_kernel, nr, nz), out_shape=[jax.S...  74.2 us
    pallas_call x1, Pallas kernels, solve(): pl.pallas_call(solve_kernel, out_shape=[jax.ShapeDtypeStruct(r.shape, F32...  6.48 us

profile of v7, /device:TPU:4, one launch (start us, length us, event | category | flops | bytes accessed | tf_op | source)
XLA Modules:
  0.0 81.5 jit_solution(10932208508668006502)
XLA Ops:
  0.6 74.2 %shard_map.59 = (f32[128,512]{1,0:T(8,128)}, f32[128,512]{1,0:T(8,128)}, f32[128,128]{1,0:T(8,128)}, f32[8,128]{1,0:T(8,128)}) custom-call(s32[8,7]{1,0:T(8,128)} %cols_in.1, f32[8,7,64,64]{3,2,1,0:T(8,128)} %tiles.1, f32[8,512]{1,0:T(8,128)} %r_in.3, f32[8,64,64]{2,1,0:T(8,128)} %pivots_in.1), custom_call_target="tpu_custom_call" | custom-call | tf_op jit(solution)/shard_map/pallas_call | solution.py:656
  74.8 6.5 %shard_map.60 = (f32[8,512]{1,0:T(8,128)}, f32[8,512]{1,0:T(8,128)}) custom-call(f32[128,128]{1,0:T(8,128)} %get-tuple-element.6.k_in, f32[8,128]{1,0:T(8,128)} %get-tuple-element.7.rt_in, f32[128,512]{1,0:T(8,128)} %get-tuple-element.8.v_in, f32[128,512]{1,0:T(8,128)} %get-tuple-element.9.w_in, f32[8,512]{1,0:T(8,128)} %r_in.3), custom_call_target="tpu_custom_call" | custom-call | tf_op jit(solution)/shard_map/pallas_call | solution.py:748

commit v8 on v7

--- a/solution.py
+++ b/solution.py
@@ -61,8 +61,8 @@
     va, wa, c, sv, other, third, joint,
     u_src, u_dst, s_src, s_dst, k_src, k_dst, w_src, w_dst, far, above, below,
     g_src, g_dst, h_dst, e_src, e_dst,
-    red_x, red_y, red_z,
-    tile_sem, in_sem, link_send, link_recv, pair_send, pair_recv,
+    red_x, red_y, red_z, rt,
+    tile_sem, in_sem, out_sem, link_send, link_recv, pair_send, pair_recv,
     z_send, z_recv, x_send, x_recv, y_send, y_recv, k_send, k_recv,
 ):
     me, mz = lax.axis_index("rows"), lax.axis_index("rhs")
@@ -597,19 +597,22 @@
     for s in over_y:
         s.wait_recv()
     both = total(red_y, ny)
-    r_out[...] = both[16:24]
     red_z[mz] = both[0:16]
+    before = list(begun)
     over_z = spread(red_z, mz, k_send, k_recv, z_peer, nz)
     begin(over_z)
+    rt[...] = both[16:24]
+    results = [
+        pltpu.make_async_copy(src, dst, out_sem.at[i])
+        for i, (src, dst) in enumerate(((red_z, k_out), (rt, r_out), (va, v_out), (wa, w_out)))
+    ]
+    results[1].start()
+    results[2].start()
     for m in range(2):
         for s in to_z(wa, m, 2 * m + 1):
             s.wait_recv()
-    v_out[...] = va[...].reshape(nz * 16, cells)
-    w_out[...] = wa[...].reshape(nz * 16, cells)
-    for s in over_z:
-        s.wait_recv()
-    k_out[...] = red_z[...].reshape(nz * 16, nz * 16)
-    for s in begun:
+    results[3].start()
+    for s in before:
         s.wait_send()
 
     @pl.when(odd & ahead)
@@ -644,6 +647,14 @@
             def _():
                 at[name].wait_send()
 
+    for s in over_z:
+        s.wait_recv()
+    results[0].start()
+    for s in over_z:
+        s.wait_send()
+    for f in results:
+        f.wait()
+
 
 def krylov(nr, nz, cols, tiles, r, pivots):
     rhs, cells = r.shape
@@ -656,13 +667,13 @@
     return pl.pallas_call(
         functools.partial(krylov_kernel, nr, nz),
         out_shape=[
-            jax.ShapeDtypeStruct((every, cells), F32),
-            jax.ShapeDtypeStruct((every, cells), F32),
-            jax.ShapeDtypeStruct((every, every), F32),
+            jax.ShapeDtypeStruct((nz, 2, rhs, cells), F32),
+            jax.ShapeDtypeStruct((nz, 2, rhs, cells), F32),
+            jax.ShapeDtypeStruct((nz, 2 * rhs, every), F32),
             jax.ShapeDtypeStruct((rhs, every), F32),
         ],
         in_specs=[pl.BlockSpec(memory_space=pltpu.HBM)] * 4,
-        out_specs=[VMEM] * 4,
+        out_specs=[pl.BlockSpec(memory_space=pltpu.HBM)] * 4,
         scratch_shapes=[pltpu.SMEM(cols.shape, jnp.int32), vector, pltpu.VMEM(pivots.shape, F32)]
         + [pltpu.VMEM(tiles.shape, F32), pltpu.VMEM((3 * cells, cells), F32)]
         + [pltpu.VMEM((3 * cells, cells), BF)] * 3
@@ -676,8 +687,9 @@
             pltpu.VMEM((SPAN, 3 * rhs, every), F32),
             pltpu.VMEM((ny, 3 * rhs, every), F32),
             pltpu.VMEM((nz, 2 * rhs, every), F32),
+            pltpu.VMEM((rhs, every), F32),
         ]
-        + [dma((tiles.shape[0],)), dma((3,))]
+        + [dma((tiles.shape[0],)), dma((3,)), dma((4,))]
         + [dma((10, 2))] * 2
         + [dma((4,))] * 2
         + [dma((4, max(nz - 1, 1)))] * 2
@@ -726,8 +738,8 @@
     for f in fetch:
         f.start()
     fetch[0].wait()
-    size = k_buf.shape[0]
-    k = k_buf[...]
+    size, cells = rt.shape[1], r.shape[1]
+    k = k_buf[...].reshape(size, size)
     kt = k.T
     row_of = lax.broadcasted_iota(jnp.int32, (size, 1), 0)
     col_of = lax.broadcasted_iota(jnp.int32, (1, size), 1)
@@ -739,8 +751,8 @@
     for f in fetch[1:]:
         f.wait()
     c = jnp.dot(rt[...], inverse, precision=high, preferred_element_type=F32)
-    x_out[...] = jnp.dot(c, v[...], precision=high, preferred_element_type=F32)
-    r_out[...] = r[...] - jnp.dot(c, w[...], precision=high, preferred_element_type=F32)
+    x_out[...] = jnp.dot(c, v[...].reshape(size, cells), precision=high, preferred_element_type=F32)
+    r_out[...] = r[...] - jnp.dot(c, w[...].reshape(size, cells), precision=high, preferred_element_type=F32)
 
 
 def solve(k, rt, v, w, r):

time: 81.6 us -> 81.4 us (level)
  no operation moved by 1% of the time
where the time goes in v8:
time: 81.4 us; the launch traced here: 81.2 us
  Pallas kernels  80.4 us (99%)
    pallas_call x1, Pallas kernels, krylov(): pl.pallas_call(functools.partial(krylov_kernel, nr, nz), out_shape=[jax.S...  73.9 us
    pallas_call x1, Pallas kernels, solve(): pl.pallas_call(solve_kernel, out_shape=[jax.ShapeDtypeStruct(r.shape, F32...  6.48 us

profile of v8, /device:TPU:4, one launch (start us, length us, event | category | flops | bytes accessed | tf_op | source)
XLA Modules:
  0.0 81.2 jit_solution(16823936285401492036)
XLA Ops:
  0.6 73.9 %shard_map.59 = (f32[8,2,8,512]{3,2,1,0:T(8,128)}, f32[8,2,8,512]{3,2,1,0:T(8,128)}, f32[8,16,128]{2,1,0:T(8,128)}, f32[8,128]{1,0:T(8,128)}) custom-call(s32[8,7]{1,0:T(8,128)} %cols_in.1, f32[8,7,64,64]{3,2,1,0:T(8,128)} %tiles.1, f32[8,512]{1,0:T(8,128)} %r_in.3, f32[8,64,64]{2,1,0:T(8,128)} %pivots_in.1), custom_call_target="tpu_custom_call" | custom-call | tf_op jit(solution)/shard_map/pallas_call | solution.py:667
  74.6 6.5 %shard_map.60 = (f32[8,512]{1,0:T(8,128)}, f32[8,512]{1,0:T(8,128)}) custom-call(f32[8,16,128]{2,1,0:T(8,128)} %get-tuple-element.6.k_in, f32[8,128]{1,0:T(8,128)} %get-tuple-element.7.rt_in, f32[8,2,8,512]{3,2,1,0:T(8,128)} %get-tuple-element.8.v_in, f32[8,2,8,512]{3,2,1,0:T(8,128)} %get-tuple-element.9.w_in, f32[8,512]{1,0:T(8,128)} %r_in.3), custom_call_target="tpu_custom_call" | custom-call | tf_op jit(solution)/shard_map/pallas_call | solution.py:760

commit v9 on v8

--- a/solution.py
+++ b/solution.py
@@ -61,7 +61,7 @@
     va, wa, c, sv, other, third, joint,
     u_src, u_dst, s_src, s_dst, k_src, k_dst, w_src, w_dst, far, above, below,
     g_src, g_dst, h_dst, e_src, e_dst,
-    red_x, red_y, red_z, rt,
+    mine, theirs, red_x, red_y, red_z, rt,
     tile_sem, in_sem, out_sem, link_send, link_recv, pair_send, pair_recv,
     z_send, z_recv, x_send, x_recv, y_send, y_recv, k_send, k_recv,
 ):
@@ -543,12 +543,26 @@
                     s.wait_recv()
             left = jnp.concatenate([wa[mz, 0], far[0], r[...]], axis=0)
             right = va[...].reshape(nz * 16, cells)
-            red_x[pos] = lax.dot_general(
+            mine[...] = lax.dot_general(
                 left, right, (((1,), (1,)), ((), ())),
                 precision=lax.Precision.HIGHEST, preferred_element_type=F32,
             )
-            over_x = spread(red_x, pos, x_send, x_recv, x_peer, SPAN)
-            begin(over_x)
+            to_odd = copy(mine, theirs, pair_send.at[4], pair_recv.at[4], (me + 1, mz))
+            over_x = [
+                copy(red_x.at[chip], red_x.at[chip], x_send.at[o - 1], x_recv.at[o - 1], x_peer(2 * o))
+                for o in range(1, chips)
+            ]
+
+            @pl.when(even)
+            def _():
+                to_odd.start()
+
+            @pl.when(odd)
+            def _():
+                to_odd.wait_recv()
+                red_x[chip] = theirs[...] + mine[...]
+                for s in over_x:
+                    s.start()
 
         @pl.when(to_next)
         def _():
@@ -589,24 +603,33 @@
             value = value + array[i]
         return value
 
-    for s in over_x:
-        s.wait_recv()
-    red_y[where] = total(red_x, SPAN)
+    before = list(begun)
     over_y = spread(red_y, where, y_send, y_recv, y_peer, ny)
-    begin(over_y)
-    for s in over_y:
-        s.wait_recv()
-    both = total(red_y, ny)
-    red_z[mz] = both[0:16]
-    before = list(begun)
     over_z = spread(red_z, mz, k_send, k_recv, z_peer, nz)
-    begin(over_z)
-    rt[...] = both[16:24]
+    to_even = [
+        copy(ref, ref, pair_send.at[5 + i], pair_recv.at[5 + i], (me - 1, mz)) for i, ref in enumerate((red_z, rt))
+    ]
+
+    @pl.when(odd)
+    def _():
+        for s in over_x:
+            s.wait_recv()
+        red_y[where] = total(red_x, chips)
+        for s in over_y:
+            s.start()
+        for s in over_y:
+            s.wait_recv()
+        both = total(red_y, ny)
+        red_z[mz] = both[0:16]
+        for s in over_z:
+            s.start()
+        rt[...] = both[16:24]
+        to_even[1].start()
+
     results = [
         pltpu.make_async_copy(src, dst, out_sem.at[i])
         for i, (src, dst) in enumerate(((red_z, k_out), (rt, r_out), (va, v_out), (wa, w_out)))
     ]
-    results[1].start()
     results[2].start()
     for m in range(2):
         for s in to_z(wa, m, 2 * m + 1):
@@ -647,11 +670,29 @@
             def _():
                 at[name].wait_send()
 
-    for s in over_z:
-        s.wait_recv()
+    @pl.when(odd)
+    def _():
+        for s in over_z:
+            s.wait_recv()
+        to_even[0].start()
+
+    @pl.when(even)
+    def _():
+        for s in to_even:
+            s.wait_recv()
+
     results[0].start()
-    for s in over_z:
-        s.wait_send()
+    results[1].start()
+
+    @pl.when(odd)
+    def _():
+        for s in over_x + over_y + over_z + to_even:
+            s.wait_send()
+
+    @pl.when(even)
+    def _():
+        to_odd.wait_send()
+
     for f in results:
         f.wait()
 
@@ -684,14 +725,16 @@
         + [square, square, pltpu.VMEM((8, cells, cells), BF)]
         + [vectors] * 16
         + [
-            pltpu.VMEM((SPAN, 3 * rhs, every), F32),
+            pltpu.VMEM((3 * rhs, every), F32),
+            pltpu.VMEM((3 * rhs, every), F32),
+            pltpu.VMEM((SPAN // 2, 3 * rhs, every), F32),
             pltpu.VMEM((ny, 3 * rhs, every), F32),
             pltpu.VMEM((nz, 2 * rhs, every), F32),
             pltpu.VMEM((rhs, every), F32),
         ]
         + [dma((tiles.shape[0],)), dma((3,)), dma((4,))]
         + [dma((10, 2))] * 2
-        + [dma((4,))] * 2
+        + [dma((7,))] * 2
         + [dma((4, max(nz - 1, 1)))] * 2
         + [dma((SPAN - 1,))] * 2
         + [dma((max(ny - 1, 1),))] * 2

time: 81.4 us -> 80.1 us (0.984)
  Pallas kernels: 80.4 us -> 79.2 us
    pallas_call x1, Pallas kernels: 73.9 us -> 72.7 us  [krylov(): pl.pallas_call(functools.partial(krylov_kernel, nr, nz), out_shape=[jax.S...]
where the time goes in v9:
time: 80.1 us; the launch traced here: 80 us
  Pallas kernels  79.2 us (99%)
    pallas_call x1, Pallas kernels, krylov(): pl.pallas_call(functools.partial(krylov_kernel, nr, nz), out_shape=[jax.S...  72.7 us
    pallas_call x1, Pallas kernels, solve(): pl.pallas_call(solve_kernel, out_shape=[jax.ShapeDtypeStruct(r.shape, F32...  6.48 us

profile of v9, /device:TPU:4, one launch (start us, length us, event | category | flops | bytes accessed | tf_op | source)
XLA Modules:
  0.0 80.0 jit_solution(15266841551829718502)
XLA Ops:
  0.6 72.7 %shard_map.59 = (f32[8,2,8,512]{3,2,1,0:T(8,128)}, f32[8,2,8,512]{3,2,1,0:T(8,128)}, f32[8,16,128]{2,1,0:T(8,128)}, f32[8,128]{1,0:T(8,128)}) custom-call(s32[8,7]{1,0:T(8,128)} %cols_in.1, f32[8,7,64,64]{3,2,1,0:T(8,128)} %tiles.1, f32[8,512]{1,0:T(8,128)} %r_in.3, f32[8,64,64]{2,1,0:T(8,128)} %pivots_in.1), custom_call_target="tpu_custom_call" | custom-call | tf_op jit(solution)/shard_map/pallas_call | solution.py:708
  73.3 6.5 %shard_map.60 = (f32[8,512]{1,0:T(8,128)}, f32[8,512]{1,0:T(8,128)}) custom-call(f32[8,16,128]{2,1,0:T(8,128)} %get-tuple-element.6.k_in, f32[8,128]{1,0:T(8,128)} %get-tuple-element.7.rt_in, f32[8,2,8,512]{3,2,1,0:T(8,128)} %get-tuple-element.8.v_in, f32[8,2,8,512]{3,2,1,0:T(8,128)} %get-tuple-element.9.w_in, f32[8,512]{1,0:T(8,128)} %r_in.3), custom_call_target="tpu_custom_call" | custom-call | tf_op jit(solution)/shard_map/pallas_call | solution.py:803

commit v10 on v9

--- a/solution.py
+++ b/solution.py
@@ -485,16 +485,17 @@
             w_src[m] = times(c[...], values(t_refs))
             at["w"].start()
 
-        @pl.when(has_before)
-        def _():
-            at["back"].start()
-
-        @pl.when(has_next)
-        def _():
-            at["on"].start()
-
         if m == 1:
             begin(to_z(va, 1, 2))
+
+        @pl.when(has_before)
+        def _():
+            at["back"].start()
+
+        @pl.when(has_next)
+        def _():
+            at["on"].start()
+
 
         if m == 0:
 

time: 80.1 us -> 80.1 us (level)
  no operation moved by 1% of the time
where the time goes in v10:
time: 80.1 us; the launch traced here: 79.9 us
  Pallas kernels  79.2 us (99%)
    pallas_call x1, Pallas kernels, krylov(): pl.pallas_call(functools.partial(krylov_kernel, nr, nz), out_shape=[jax.S...  72.7 us
    pallas_call x1, Pallas kernels, solve(): pl.pallas_call(solve_kernel, out_shape=[jax.ShapeDtypeStruct(r.shape, F32...  6.48 us

profile of v10, /device:TPU:4, one launch (start us, length us, event | category | flops | bytes accessed | tf_op | source)
XLA Modules:
  0.0 79.9 jit_solution(10311439870945557432)
XLA Ops:
  0.6 72.7 %shard_map.59 = (f32[8,2,8,512]{3,2,1,0:T(8,128)}, f32[8,2,8,512]{3,2,1,0:T(8,128)}, f32[8,16,128]{2,1,0:T(8,128)}, f32[8,128]{1,0:T(8,128)}) custom-call(s32[8,7]{1,0:T(8,128)} %cols_in.1, f32[8,7,64,64]{3,2,1,0:T(8,128)} %tiles.1, f32[8,512]{1,0:T(8,128)} %r_in.3, f32[8,64,64]{2,1,0:T(8,128)} %pivots_in.1), custom_call_target="tpu_custom_call" | custom-call | tf_op jit(solution)/shard_map/pallas_call | solution.py:709
  73.3 6.5 %shard_map.60 = (f32[8,512]{1,0:T(8,128)}, f32[8,512]{1,0:T(8,128)}) custom-call(f32[8,16,128]{2,1,0:T(8,128)} %get-tuple-element.6.k_in, f32[8,128]{1,0:T(8,128)} %get-tuple-element.7.rt_in, f32[8,2,8,512]{3,2,1,0:T(8,128)} %get-tuple-element.8.v_in, f32[8,2,8,512]{3,2,1,0:T(8,128)} %get-tuple-element.9.w_in, f32[8,512]{1,0:T(8,128)} %r_in.3), custom_call_target="tpu_custom_call" | custom-call | tf_op jit(solution)/shard_map/pallas_call | solution.py:804
